TPU v7x, 128 devices: a whole 4x4x4 slice. The times are simulated.
128 devices in a mesh: side: 2 (over y_hi), dev: 64 (over y_lo, z, x, core).
Axes of the slice: x: 4, y: 4 (y_hi: 2, y_lo: 2; y = y_hi * 2 + y_lo), z: 4, core: 2. Of those that a mesh axis runs over, the one named last changes fastest.
Arguments:
- queries: bfloat16 [2048, 8192], P('dev', 'side'), may hold values from -6 to 6
- cache_keys: bfloat16 [2048, 256, 512], P('dev', None, 'side'), may hold values from -6 to 6
- cache_values: bfloat16 [2048, 256, 512], P('dev', None, 'side'), may hold values from -6 to 6
- new_key: bfloat16 [2048, 512], P('dev', 'side'), may hold values from -15 to 15
- new_value: bfloat16 [2048, 512], P('dev', 'side'), may hold values from -6 to 6
- cache_lengths: int32 [2048], P('dev'), may hold values from 2 to 256, as said below
- hidden: bfloat16 [2048, 4096], P('dev'), may hold values from -6 to 6
- norm_gain: bfloat16 [4096], replicated, may hold values from 0.099609375 to 1.8984375
- expert_ids: int32 [2048, 8], P('dev'), may hold values from 0 to 63, all different within a row; in each aligned block of 32 rows (0 to 31, 32 to 63, ...) at most 8 rows name the same one
- router_probs: float32 [2048, 8], P('dev'), may hold values from 0.02 to 1
- w_gate: bfloat16 [64, 4096, 1536], P('dev', None, 'side'), may hold values from -0.09375 to 0.09375
- w_up: bfloat16 [64, 4096, 1536], P('dev', None, 'side'), may hold values from -0.09375 to 0.09375
- w_down: bfloat16 [64, 1536, 4096], P('dev', 'side'), may hold values from -0.15625 to 0.15625
Outputs:
- context: bfloat16 [2048, 8192], P('dev', 'side')
- moe_out: bfloat16 [2048, 4096], P('dev')
Inputs may be any that keep to these rules, and one draw needn't show every extreme that they name: `expert_ids`: in each aligned block of 32 rows (the rows of one dev index) no expert is named more than 8 times, a bound that some block reaches. `cache_lengths`: every aligned block of 32 tokens holds a token with 256 valid positions.
All inputs are finite; a program needn't handle non-finite values.
Results may differ from a plain program's by a relative error of at most 0.012.
Values may be sent and summed in bfloat16 or wider, within the bound.
A program may use at most 128 MiB of HBM per device.

v0:
```python
import jax
import jax.numpy as jnp
from jax import lax
from jax.sharding import PartitionSpec as P

HEADS = 64
KV_HEADS = 4
HEAD_DIM = 128


def route_onehot(block_ids, expert_count, capacity):
    flat_ids = block_ids.reshape(-1)
    expert_hot = (flat_ids[:, None] == jnp.arange(expert_count, dtype=jnp.int32)[None, :]).astype(
        jnp.int32
    )
    earlier = jnp.cumsum(expert_hot, axis=0) - expert_hot
    slot_rank = jnp.sum(earlier * expert_hot, axis=1)
    slot_hot = (slot_rank[:, None] == jnp.arange(capacity, dtype=jnp.int32)[None, :]).astype(
        jnp.float32
    )
    route_hot = expert_hot.astype(jnp.float32)[:, :, None] * slot_hot[:, None, :]
    return route_hot.reshape(block_ids.shape[0], block_ids.shape[1], expert_count, capacity)


def attend_local(queries, cache_keys, cache_values, new_key, new_value, cache_lengths):
    row_count = queries.shape[0]
    cache_len = cache_keys.shape[1]
    groups = cache_keys.shape[2] // HEAD_DIM
    per_group = HEADS // KV_HEADS
    score_scale = HEAD_DIM ** (-0.5)
    query_heads = queries.reshape(row_count, groups, per_group, HEAD_DIM)
    key_heads = cache_keys.reshape(row_count, cache_len, groups, HEAD_DIM)
    value_heads = cache_values.reshape(row_count, cache_len, groups, HEAD_DIM)
    scores = (
        jnp.einsum("tgqd,tlgd->tgql", query_heads, key_heads, preferred_element_type=jnp.float32)
        * score_scale
    )
    own_key = new_key.reshape(row_count, groups, HEAD_DIM)
    own_score = (
        jnp.einsum("tgqd,tgd->tgq", query_heads, own_key, preferred_element_type=jnp.float32)
        * score_scale
    )
    visible = jnp.arange(cache_len, dtype=jnp.int32)[None, :] < cache_lengths[:, None]
    scores = jnp.where(visible[:, None, None, :], scores, -1e30)
    top_score = jnp.maximum(jnp.max(scores, axis=3), own_score)
    exp_scores = jnp.exp(scores - top_score[..., None])
    own_exp = jnp.exp(own_score - top_score)
    denominator = jnp.sum(exp_scores, axis=3) + own_exp
    attn_weights = (exp_scores / denominator[..., None]).astype(jnp.bfloat16)
    own_prob = (own_exp / denominator).astype(jnp.bfloat16)
    combined = jnp.einsum(
        "tgql,tlgd->tgqd", attn_weights, value_heads, preferred_element_type=jnp.float32
    )
    own_value = new_value.reshape(row_count, groups, 1, HEAD_DIM).astype(jnp.float32)
    combined = combined + own_prob.astype(jnp.float32)[..., None] * own_value
    return combined.reshape(row_count, groups * per_group * HEAD_DIM).astype(jnp.bfloat16)


def per_device(
    queries,
    cache_keys,
    cache_values,
    new_key,
    new_value,
    cache_lengths,
    hidden,
    norm_gain,
    expert_ids,
    router_probs,
    w_gate,
    w_up,
    w_down,
):
    context = attend_local(queries, cache_keys, cache_values, new_key, new_value, cache_lengths)
    row_count = hidden.shape[0]
    top_count = expert_ids.shape[1]
    devices = lax.axis_size("dev")
    experts = w_gate.shape[0] * devices
    capacity = max(2, 2 * row_count * top_count // experts)
    gate_share = router_probs / jnp.sum(router_probs, axis=1, keepdims=True)
    hidden_wide = hidden.astype(jnp.float32)
    inverse = lax.rsqrt(jnp.mean(hidden_wide * hidden_wide, axis=1, keepdims=True) + 1e-06)
    normed = (hidden_wide * inverse * norm_gain.astype(jnp.float32)[None, :]).astype(jnp.bfloat16)
    route_hot = route_onehot(expert_ids, experts, capacity)
    slot_hot = jnp.sum(route_hot, axis=1)
    slot_gate = jnp.sum(route_hot * gate_share[:, :, None, None], axis=1)
    buffer = jnp.einsum(
        "rec,rd->ecd", slot_hot.astype(jnp.bfloat16), normed, preferred_element_type=jnp.float32
    ).astype(jnp.bfloat16)
    row_block = lax.all_to_all(buffer, "dev", split_axis=0, concat_axis=0, tiled=True)
    gate_act = jnp.einsum("scd,df->scf", row_block, w_gate[0], preferred_element_type=jnp.float32)
    up_act = jnp.einsum("scd,df->scf", row_block, w_up[0], preferred_element_type=jnp.float32)
    activation = (jax.nn.silu(gate_act) * up_act).astype(jnp.bfloat16)
    partial_out = jnp.einsum(
        "scf,fd->scd", activation, w_down[0], preferred_element_type=jnp.float32
    ).astype(jnp.bfloat16)
    back = lax.all_to_all(partial_out, "dev", split_axis=0, concat_axis=0, tiled=True)
    local_mix = jnp.einsum(
        "rec,ecd->rd", slot_gate, back.astype(jnp.float32), precision=lax.Precision.HIGHEST
    )
    combined = lax.psum(local_mix, "side")
    return (context, combined.astype(jnp.bfloat16))


def solution(mesh):
    in_specs = (
        P("dev", "side"),
        P("dev", None, "side"),
        P("dev", None, "side"),
        P("dev", "side"),
        P("dev", "side"),
        P("dev"),
        P("dev", None),
        P(),
        P("dev", None),
        P("dev", None),
        P("dev", None, "side"),
        P("dev", None, "side"),
        P("dev", "side", None),
    )
    out_specs = (P("dev", "side"), P("dev", None))
    return jax.shard_map(
        per_device, mesh=mesh, in_specs=in_specs, out_specs=out_specs, check_vma=False
    )
```

profile of v0, /device:TPU:2, one launch (start us, length us, event | category | flops | bytes accessed | tf_op | source)
XLA Modules:
  0.0 173.4 jit_solution(5468898151774488935)
XLA Ops:
  0.6 0.8 copy.38
  1.7 0.6 reduce-window.6
  2.3 0.2 slice_reduce_fusion
  2.9 0.7 reduce_sum.56
  3.6 0.7 broadcast_divide_fusion
  4.3 0.7 multiply_reduce_fusion
  5.2 0.7 convert_element_type.92
  5.9 1.1 fusion.32
  7.0 2.4 %convolution_convert_fusion = bf16[64,8,4096]{2,1,0:T(8,128)(2,1)S(1)} fusion(bf16[32,64,8]{0,2,1:T(8,128)(2,1)S(1)} %copy.43, bf16[32,4096]{1,0:T(8,128)(2,1)} %param.19, f32[4096]{0:T(1024)S(1)} %convert_element_type.92, f32[32]{0:T(128)S(1)} %add_rsqrt_fusion), kind=kOutput, calls=%fused_computation.7 | convolution fusion | flops 136839168 | bytes 4505728 | tf_op jit(solution)/shard_map/rec,rd->ecd/dot_general | solution.py:87
  9.5 61.6 %all_to_all.10 = bf16[64,8,4096]{2,1,0:T(8,128)(2,1)S(1)} all-to-all(bf16[64,8,4096]{2,1,0:T(8,128)(2,1)S(1)} %convolution_convert_fusion), channel_id=1, replica_groups=mesh['side'=2,'dev'=64] {'dev'}, dimensions={0} | all-to-all | bytes 8388608 | tf_op jit(solution)/shard_map/all_to_all | solution.py:90
  71.1 3.5 %fusion.4 = f32[64,8,768]{2,1,0:T(8,128)S(1)} fusion(bf16[64,8,4096]{2,1,0:T(8,128)(2,1)S(1)} %all_to_all.10, bf16[1,4096,768]{2,1,0:T(8,128)(2,1)S(1)} %bitcast.90), kind=kOutput, calls=%fused_computation.4 | convolution fusion | flops 3221225472 | bytes 12058624 | tf_op jit(solution)/shard_map/scd,df->scf/dot_general | solution.py:91
  74.6 3.6 %multiply_convert_fusion = bf16[64,8,768]{2,1,0:T(8,128)(2,1)S(1)} fusion(f32[64,8,768]{2,1,0:T(8,128)S(1)} %fusion.4, bf16[64,8,4096]{2,1,0:T(8,128)(2,1)S(1)} %all_to_all.10, bf16[1,4096,768]{2,1,0:T(8,128)(2,1)S(1)} %bitcast.92), kind=kOutput, calls=%fused_computation.15 | convolution fusion | flops 3223584768 | bytes 12845056 | tf_op jit(solution)/shard_map/scd,df->scf/dot_general | solution.py:92
  78.2 3.7 %fusion.6 = bf16[64,8,4096]{2,0,1:T(8,128)(2,1)S(1)} fusion(bf16[1,768,4096]{2,1,0:T(8,128)(2,1)S(1)} %bitcast.94, bf16[64,8,768]{2,1,0:T(8,128)(2,1)S(1)} %multiply_convert_fusion), kind=kOutput, calls=%fused_computation.6 | convolution fusion | flops 3223322624 | bytes 11272192 | tf_op jit(solution)/shard_map/scf,fd->scd/dot_general | solution.py:94
  81.9 4.3 %copy.45 = bf16[64,8,4096]{2,1,0:T(8,128)(2,1)} copy(bf16[64,8,4096]{2,0,1:T(8,128)(2,1)S(1)} %fusion.6) | data formatting | bytes 8388608 | tf_op jit(solution)/shard_map/convert_element_type | solution.py:96
  86.2 5.7 %all-to-all-start.1 = ((bf16[64,8,4096]{2,1,0:T(8,128)(2,1)}), bf16[64,8,4096]{2,1,0:T(8,128)(2,1)}, u32[]{:S(2)}, u32[]{:S(2)}) async-start(bf16[64,8,4096]{2,1,0:T(8,128)(2,1)} %copy.45), calls=%async_computation.1 | async-start | bytes 8388608 | tf_op jit(solution)/shard_map/all_to_all | solution.py:97
  92.1 0.2 fusion.49
  92.3 3.7 %fusion.48 = (f32[32,2,16]{2,1,0:T(2,128)S(1)}, f32[32,2,16,256]{3,2,1,0:T(8,128)S(1)}) fusion(bf16[32,2,16,128]{3,2,1,0:T(8,128)(2,1)S(1)} %bitcast.83, pred[32,256]{1,0:T(8,128)(4,1)S(1)} %iota_compare_fusion.4, bf16[32,256,256]{2,1,0:T(8,128)(2,1)} %param.14), kind=kOutput, calls=%fused_computation.59 | convolution fusion | flops 67894272 | bytes 5517312 | tf_op jit(solution)/shard_map/tgqd,tlgd->tgql/dot_general | solution.py:35
  96.0 0.4 fusion.30
  96.6 1.0 fusion.26
  97.6 0.8 copy.80
  98.4 0.2 copy.50
  98.6 47.8 %all-to-all-done.1 = bf16[64,8,4096]{2,1,0:T(8,128)(2,1)} async-done(((bf16[64,8,4096]{2,1,0:T(8,128)(2,1)}), bf16[64,8,4096]{2,1,0:T(8,128)(2,1)}, u32[]{:S(2)}, u32[]{:S(2)}) %all-to-all-start.1) | async-done | bytes 4194336 | tf_op jit(solution)/shard_map/all_to_all | solution.py:97
  146.4 4.4 %convolution_bitcast_fusion = f32[32,4096]{1,0:T(8,128)S(1)} fusion(f32[32,64,8]{0,2,1:T(8,128)S(1)} %copy.50, bf16[64,8,4096]{2,1,0:T(8,128)(2,1)} %all-to-all-done.1), kind=kOutput, calls=%fused_computation.8 | convolution fusion | flops 805306368 | bytes 4784128 | tf_op jit(solution)/shard_map/rec,ecd->rd/dot_general | solution.py:98
  150.8 22.6 %all-reduce.1 = bf16[32,4096]{1,0:T(8,128)(2,1)} all-reduce(f32[32,4096]{1,0:T(8,128)S(1)} %convolution_bitcast_fusion), channel_id=1, replica_groups=mesh['side'=2,'dev'=64] {'side'}, use_global_device_ids=true, to_apply=%region_9.10 | all-reduce | flops 131072 | bytes 786432 | tf_op jit(solution)/shard_map/psum | solution.py:101
  (43 shorter events, 1.2 us)
Async XLA Ops:
  7.0 64.1 %slice-start = ((s8[6291456]{0:T(1024)(128)(4,1)}), s8[4194304]{0:T(1024)(128)(4,1)S(1)}, s32[]{:S(2)}) async-start(s8[6291456]{0:T(1024)(128)(4,1)} %bitcast.89), calls=%async_computation.2 | async-start | bytes 8388608
  9.4 61.7 %slice-start.1 = ((s8[6291456]{0:T(1024)(128)(4,1)}), s8[2097152]{0:T(1024)(128)(4,1)S(1)}, s32[]{:S(2)}) async-start(s8[6291456]{0:T(1024)(128)(4,1)} %bitcast.89), calls=%async_computation.3 | async-start | bytes 4194304
  9.4 65.1 %slice-start.2 = ((s8[6291456]{0:T(1024)(128)(4,1)}), s8[4194304]{0:T(1024)(128)(4,1)S(1)}, s32[]{:S(2)}) async-start(s8[6291456]{0:T(1024)(128)(4,1)} %bitcast.91), calls=%async_computation.4 | async-start | bytes 8388608
  71.1 3.5 %slice-start.3 = ((s8[6291456]{0:T(1024)(128)(4,1)}), s8[2097152]{0:T(1024)(128)(4,1)S(1)}, s32[]{:S(2)}) async-start(s8[6291456]{0:T(1024)(128)(4,1)} %bitcast.91), calls=%async_computation.5 | async-start | bytes 4194304
  71.1 7.1 %slice-start.4 = ((s8[6291456]{0:T(1024)(128)(4,1)}), s8[4194304]{0:T(1024)(128)(4,1)S(1)}, s32[]{:S(2)}) async-start(s8[6291456]{0:T(1024)(128)(4,1)} %bitcast.93), calls=%async_computation.6 | async-start | bytes 8388608
  74.6 3.6 %slice-start.5 = ((s8[6291456]{0:T(1024)(128)(4,1)}), s8[2097152]{0:T(1024)(128)(4,1)S(1)}, s32[]{:S(2)}) async-start(s8[6291456]{0:T(1024)(128)(4,1)} %bitcast.93), calls=%async_computation.7 | async-start | bytes 4194304
  86.2 5.7 %copy-start = (bf16[32,4096]{1,0:T(8,128)(2,1)S(1)}, bf16[32,4096]{1,0:T(8,128)(2,1)}, u32[]{:S(2)}) copy-start(bf16[32,4096]{1,0:T(8,128)(2,1)} %param.13) | copy-start | bytes 786436
  86.2 5.8 %copy-start.1 = (bf16[32,256]{1,0:T(8,128)(2,1)S(1)}, bf16[32,256]{1,0:T(8,128)(2,1)}, u32[]{:S(2)}) copy-start(bf16[32,256]{1,0:T(8,128)(2,1)} %param.16) | copy-start | bytes 49156
  86.2 5.8 %copy-start.2 = (bf16[32,256]{1,0:T(8,128)(2,1)S(1)}, bf16[32,256]{1,0:T(8,128)(2,1)}, u32[]{:S(2)}) copy-start(bf16[32,256]{1,0:T(8,128)(2,1)} %param.17) | copy-start | bytes 49156
  86.2 5.8 %copy-start.3 = (s32[32]{0:T(128)S(1)}, s32[32]{0:T(128)}, u32[]{:S(2)}) copy-start(s32[32]{0:T(128)} %param.18) | copy-start | bytes 388
  86.2 60.2 %all-to-all-start.1 = ((bf16[64,8,4096]{2,1,0:T(8,128)(2,1)}), bf16[64,8,4096]{2,1,0:T(8,128)(2,1)}, u32[]{:S(2)}, u32[]{:S(2)}) async-start(bf16[64,8,4096]{2,1,0:T(8,128)(2,1)} %copy.45), calls=%async_computation.1 | async-start | bytes 8388608 | tf_op jit(solution)/shard_map/all_to_all | solution.py:97
  92.0 4.6 %copy-start.4 = (bf16[32,256,256]{2,1,0:T(8,128)(2,1)S(1)}, bf16[32,256,256]{2,1,0:T(8,128)(2,1)}, u32[]{:S(2)}) copy-start(bf16[32,256,256]{2,1,0:T(8,128)(2,1)} %param.15) | copy-start | bytes 12582916
where the time goes:
time: 174 us; the launch traced here: 173 us
  blocking collectives  84.2 us (48%)
  waiting for transfers between devices  47.8 us (27%)
  matrix products  22.4 us (13%)
  local copies, waits for them, and re-layouts  6.81 us (4%)
  starting transfers between devices  5.68 us (3%)
  other arithmetic  5.51 us (3%)
    all_to_all x1, blocking collectives, per_device(): lax.all_to_all(buffer, 'dev', split_axis=0, concat_axis=0, tiled=True)  61.6 us
    all_to_all x1, waiting for transfers between devices, per_device(): lax.all_to_all(partial_out, 'dev', split_axis=0, concat_axis=0, tiled=True)  47.8 us
    psum x1, blocking collectives, per_device(): combined = lax.psum(local_mix, 'side')  22.6 us
    all_to_all x1, starting transfers between devices, per_device(): lax.all_to_all(partial_out, 'dev', split_axis=0, concat_axis=0, tiled=True)  5.68 us
    dot_general x1, matrix products, per_device(): jnp.einsum('rec,ecd->rd', slot_gate, back.astype(jnp.float32), precision=...  4.42 us
    convert_element_type x1, local copies, waits for them, and re-layouts, per_device(): partial_out = jnp.einsum('scf,fd->scd', activation, w_down[0], preferred_...  4.27 us
    dot_general x1, matrix products, attend_local(): jnp.einsum('tgqd,tlgd->tgql', query_heads, key_heads, preferred_element_t...  3.67 us
    dot_general x1, matrix products, per_device(): jnp.einsum('scf,fd->scd', activation, w_down[0], preferred_element_type=j...  3.66 us
  transfers between devices with their start and end apart: 1, of which 1 were waited for; matrix products, arithmetic and copies ran while one was open for 4% of the time, Pallas kernels for 0%

commit v1 on v0

v1 whole, which is shorter than its diff:
```python
import functools

import jax
import jax.numpy as jnp
from jax import lax
from jax.experimental import pallas as pl
from jax.experimental.pallas import tpu as pltpu
from jax.sharding import PartitionSpec as P

HEADS = 64
KV_HEADS = 4
HEAD_DIM = 128
RING = 4
BLOCKS = 16
ROWS = 32
SLOTS = 8
GROUPS = 4
D = 4096
HALF = 2048
TAIL = 128
WIDE = HALF + TAIL
MESH = pl.DeviceIdType.MESH
F32 = jnp.float32
BF16 = jnp.bfloat16


class Place:
    def __init__(self):
        self.side = lax.axis_index("side")
        dev = lax.axis_index("dev")
        self.dev = dev
        self.core = dev % 2
        self.x = (dev // 2) % RING
        self.z = (dev // 8) % RING
        self.lo = dev // 32
        self.y = self.side * 2 + self.lo

    @staticmethod
    def index(lo, z, x, core):
        return ((lo * RING + z) * RING + x) * 2 + core

    def plane(self, axis, step):
        if axis == "x":
            return (self.side, self.index(self.lo, self.z, (self.x + step) % RING, self.core))
        return (self.side, self.index(self.lo, (self.z + step) % RING, self.x, self.core))

    def along_y(self, step, core):
        y = (self.y + step) % RING
        return (y // 2, self.index(y % 2, self.z, self.x, core))

    def sibling(self):
        return (self.side, self.index(self.lo, self.z, self.x, 1 - self.core))

    def block(self, half, first, second):
        if half == 0:
            x, z = (self.x + first) % RING, (self.z + second) % RING
        else:
            z, x = (self.z + first) % RING, (self.x + second) % RING
        return z * RING + x


AXES = (("x", "z"), ("z", "x"))
NEAR = (0, -1, 1, 2)


def greet(devices):
    barrier = pltpu.get_barrier_semaphore()
    for device in devices:
        pl.semaphore_signal(barrier, inc=1, device_id=device, device_id_type=MESH)
    pl.semaphore_wait(barrier, len(devices))


def routing_table(ids_ref, probs_ref):
    lane = lax.broadcasted_iota(jnp.int32, (ROWS, TAIL), 1)
    expert = lane % 64
    ids = ids_ref[...]
    probs = probs_ref[...]
    share = probs / jnp.sum(probs, axis=1, keepdims=True)
    hit = jnp.zeros((ROWS, TAIL), F32)
    gate = jnp.zeros((ROWS, TAIL), F32)
    for k in range(ids.shape[1]):
        match = ids[:, k : k + 1] == expert
        hit = jnp.where(match, 1.0, hit)
        gate = jnp.where(match, share[:, k : k + 1], gate)
    row = lax.broadcasted_iota(jnp.int32, (ROWS, ROWS), 0)
    col = lax.broadcasted_iota(jnp.int32, (ROWS, ROWS), 1)
    before = jnp.where(col < row, 1.0, 0.0).astype(BF16)
    rank = jnp.dot(before, hit.astype(BF16), preferred_element_type=F32)
    rank = jnp.where(hit > 0.5, rank, 100.0)
    lead = gate.astype(BF16)
    trail = (gate - lead.astype(F32)).astype(BF16)
    left = lane < 64
    rank = rank.astype(BF16)
    return jnp.where(left, rank, lead), jnp.where(left, rank, trail)


def dispatch_kernel(
    hidden_ref, gain_ref, ids_ref, probs_ref, x_ref, weight_ref,
    gathered, picked_y, picked_s, ag_send, ag_recv, pick_send, x_recv,
):
    me = Place()
    own_group = me.lo * 2 + me.core

    wide = hidden_ref[...].astype(F32)
    inverse = lax.rsqrt(jnp.mean(wide * wide, axis=1, keepdims=True) + 1e-06)
    normed = (wide * inverse * gain_ref[...].astype(F32)).astype(BF16)
    tables = routing_table(ids_ref, probs_ref)
    own_block = me.block(0, 0, 0)
    for half in range(2):
        gathered[half, own_block, :, 0:HALF] = normed[:, half * HALF : (half + 1) * HALF]
        gathered[half, own_block, :, HALF:WIDE] = tables[half]

    lo = 1 - me.lo
    experts = (
        me.dev,
        me.index(me.lo, me.z, me.x, 1 - me.core),
        me.index(lo, me.z, me.x, 0),
        me.index(lo, me.z, me.x, 1),
    )
    slot_of = lax.broadcasted_iota(jnp.int32, (GROUPS * SLOTS, TAIL), 0)
    lane = lax.broadcasted_iota(jnp.int32, (GROUPS * SLOTS, TAIL), 1)
    wanted = jnp.zeros((GROUPS * SLOTS, TAIL), jnp.int32)
    for j in range(GROUPS):
        wanted = jnp.where(slot_of // SLOTS == j, experts[j], wanted)
    pick_rank = jnp.where(lane == wanted, 1.0, 0.0).astype(BF16)
    pick_gate = jnp.where(lane == wanted + 64, 1.0, 0.0).astype(BF16)

    greet(
        [me.plane(axis, step) for axis in ("x", "z") for step in (-1, 1)]
        + [me.along_y(step, core) for step in (-1, 1) for core in (0, 1)]
        + [me.sibling()]
    )

    def hop(half, block, rows, stage, step, sem):
        ref = gathered.at[half, block, rows]
        return pltpu.make_async_remote_copy(
            src_ref=ref, dst_ref=ref, send_sem=ag_send, recv_sem=ag_recv.at[half, sem],
            device_id=me.plane(AXES[half][stage], step), device_id_type=MESH,
        )

    full, low, high = pl.ds(0, ROWS), pl.ds(0, ROWS // 2), pl.ds(ROWS // 2, ROWS // 2)

    def send_both(half, first, stage, base):
        block = me.block(half, first, 0)
        hop(half, block, full, stage, 1, base).start()
        hop(half, block, full, stage, -1, base + 1).start()

    def arrive(half, block, rows, sem):
        ref = gathered.at[half, block, rows]
        pltpu.make_async_copy(ref, ref, ag_recv.at[half, sem]).wait()

    def take_full(half, first, second, stage, base):
        ahead = 1 if stage == 0 else 0
        for step, rows, sem in ((-1, low, base), (1, high, base + 1)):
            block = me.block(half, step, 0) if ahead else me.block(half, first, step)
            arrive(half, block, full, sem)
            hop(half, block, rows, stage, -step, sem + 2).start()

    def take_far(half, first, stage, base):
        block = me.block(half, 2, 0) if stage == 0 else me.block(half, first, 2)
        arrive(half, block, low, base + 2)
        arrive(half, block, high, base + 3)

    def select(half, first, second):
        block = me.block(half, first, second)
        table = gathered[half, block, :, HALF:WIDE]
        rank = lax.dot_general(pick_rank, table, (((1,), (1,)), ((), ())), preferred_element_type=F32)
        slot = (lax.broadcasted_iota(jnp.int32, (GROUPS * SLOTS, ROWS), 0) % SLOTS).astype(F32)
        hot = jnp.where(rank == slot, 1.0, 0.0).astype(BF16)
        chosen = jnp.dot(hot, gathered[half, block, :, 0:HALF], preferred_element_type=F32).astype(BF16)
        columns = pl.ds(half * HALF, HALF)
        x_ref[own_group, block, :, columns] = chosen[0:8]
        picked_s[half, block] = chosen[8:16]
        picked_y[half, block, 0] = chosen[16:24]
        picked_y[half, block, 1] = chosen[24:32]
        for core in range(2):
            pltpu.make_async_remote_copy(
                src_ref=picked_y.at[half, block, core],
                dst_ref=x_ref.at[own_group, block, :, columns],
                send_sem=pick_send, recv_sem=x_recv,
                device_id=me.along_y(1 if half == 0 else -1, core), device_id_type=MESH,
            ).start()
        pltpu.make_async_remote_copy(
            src_ref=picked_s.at[half, block],
            dst_ref=x_ref.at[own_group, block, :, columns],
            send_sem=pick_send, recv_sem=x_recv,
            device_id=me.sibling(), device_id_type=MESH,
        ).start()

    both = range(2)
    for half in both:
        send_both(half, 0, 0, 0)
    for half in both:
        send_both(half, 0, 1, 4)
    for half in both:
        select(half, 0, 0)
    for half in both:
        take_full(half, 0, 0, 0, 0)
        send_both(half, -1, 1, 8)
        send_both(half, 1, 1, 12)
    for half in both:
        select(half, -1, 0)
        select(half, 1, 0)
    for half in both:
        take_full(half, 0, 0, 1, 4)
    for half in both:
        take_far(half, 0, 0, 0)
        send_both(half, 2, 1, 16)
    for half in both:
        select(half, 0, -1)
        select(half, 0, 1)
        select(half, 2, 0)
    for index in range(1, 4):
        first = NEAR[index]
        for half in both:
            take_full(half, first, 0, 1, 4 + 4 * index)
        for half in both:
            take_far(half, NEAR[index - 1], 1, 4 * index)
        for half in both:
            select(half, NEAR[index - 1], 2)
            select(half, first, -1)
            select(half, first, 1)
    for half in both:
        take_far(half, 2, 1, 16)
        select(half, 2, 2)

    for block in range(BLOCKS):
        rank = lax.dot_general(
            gathered[0, block, :, HALF:WIDE], pick_rank, (((1,), (1,)), ((), ())), preferred_element_type=F32
        )
        gate = sum(
            lax.dot_general(
                gathered[half, block, :, HALF:WIDE], pick_gate, (((1,), (1,)), ((), ())), preferred_element_type=F32
            )
            for half in both
        )
        slot = (lax.broadcasted_iota(jnp.int32, (ROWS, GROUPS * SLOTS), 1) % SLOTS).astype(F32)
        weight_ref[block] = jnp.where(rank == slot, gate, 0.0)

    sent = gathered.at[:, pl.ds(0, 15)]
    pltpu.make_async_copy(sent, sent, ag_send).wait()
    picked = picked_y.at[...]
    pltpu.make_async_copy(picked, picked, pick_send).wait()
    picked = picked_s.at[...]
    pltpu.make_async_copy(picked, picked, pick_send).wait()
    came = x_ref.at[pl.ds(0, 3)]
    pltpu.make_async_copy(came, came, x_recv).wait()


def dispatch(hidden, gain, ids, probs):
    vmem = pl.BlockSpec(memory_space=pltpu.VMEM)
    return pl.pallas_call(
        dispatch_kernel,
        out_shape=(
            jax.ShapeDtypeStruct((GROUPS, BLOCKS, SLOTS, D), BF16),
            jax.ShapeDtypeStruct((BLOCKS, ROWS, GROUPS * SLOTS), F32),
        ),
        in_specs=[vmem] * 4,
        out_specs=(vmem, vmem),
        scratch_shapes=[
            pltpu.VMEM((2, BLOCKS, ROWS, WIDE), BF16),
            pltpu.VMEM((2, BLOCKS, 2, SLOTS, HALF), BF16),
            pltpu.VMEM((2, BLOCKS, SLOTS, HALF), BF16),
            pltpu.SemaphoreType.DMA,
            pltpu.SemaphoreType.DMA((2, 20)),
            pltpu.SemaphoreType.DMA,
            pltpu.SemaphoreType.DMA,
        ],
        compiler_params=pltpu.CompilerParams(
            collective_id=0, has_side_effects=True, vmem_limit_bytes=40 * 1024 * 1024
        ),
        name="dispatch",
    )(hidden, gain, ids, probs)


def combine_kernel(
    out_ref_in, weight_ref, moe_ref,
    landed, far2_out, near2_out, far2_in, near2_in, far1_out, near1_out, far1_in, near1_in,
    side_out, side_in,
    land_send, land_recv, ring_send, far2_recv, near2_recv, far1_recv, near1_recv, side_send, side_recv,
):
    me = Place()
    lo = 1 - me.lo
    both = range(2)
    order = (2, 1, -1, 0)
    step2 = (2, 1, -1, 0)

    other_side = (1 - me.side, me.dev)
    greet(
        [me.plane(axis, step) for axis in ("x", "z") for step in (-1, 1)]
        + [me.along_y(step, core) for step in (-1, 1) for core in (0, 1)]
        + [me.sibling(), other_side]
    )

    for first in order:
        for second in step2:
            for half in both:
                block = me.block(half, first, second)
                columns = pl.ds(half * HALF, HALF)
                for core in range(2):
                    pltpu.make_async_remote_copy(
                        src_ref=out_ref_in.at[lo * 2 + core, block, :, columns],
                        dst_ref=landed.at[half, block, 1 + me.core],
                        send_sem=land_send, recv_sem=land_recv.at[half, block],
                        device_id=me.along_y(1 if half == 0 else -1, core), device_id_type=MESH,
                    ).start()
                pltpu.make_async_remote_copy(
                    src_ref=out_ref_in.at[me.lo * 2 + 1 - me.core, block, :, columns],
                    dst_ref=landed.at[half, block, 0],
                    send_sem=land_send, recv_sem=land_recv.at[half, block],
                    device_id=me.sibling(), device_id_type=MESH,
                ).start()

    own_group = me.lo * 2 + me.core

    def mixed(half, first, second):
        block = me.block(half, first, second)
        ref = landed.at[half, block]
        pltpu.make_async_copy(ref, ref, land_recv.at[half, block]).wait()
        weight = weight_ref[block]
        lead = weight.astype(BF16)
        trail = (weight - lead.astype(F32)).astype(BF16)
        own = out_ref_in[own_group, block, :, pl.ds(half * HALF, HALF)]
        parts = landed[half, block]
        rows = jnp.concatenate([own, parts[0], parts[1], parts[2]], axis=0)
        return jnp.dot(lead, rows, preferred_element_type=F32) + jnp.dot(trail, rows, preferred_element_type=F32)

    def ring(half, stage, step, src, dst, sem):
        pltpu.make_async_remote_copy(
            src_ref=src, dst_ref=dst, send_sem=ring_send, recv_sem=sem,
            device_id=me.plane(AXES[half][stage], step), device_id_type=MESH,
        ).start()

    def arrive(ref, sem):
        pltpu.make_async_copy(ref, ref, sem).wait()

    low, high = slice(0, ROWS // 2), slice(ROWS // 2, ROWS)
    def send_far(half, stage, value, out, into, sems):
        out[...] = value.astype(BF16)
        for way, step, rows in ((0, 1, pl.ds(0, 16)), (1, -1, pl.ds(16, 16))):
            ring(half, stage, step, out.at[rows], into.at[way], sems(way))

    def send_near(half, stage, way, value, far_in, far_sem, out, into, sem):
        arrive(far_in, far_sem)
        passed = far_in[...].astype(F32)
        if way == 0:
            out[low] = (value[low] + passed).astype(BF16)
            out[high] = value[high].astype(BF16)
        else:
            out[low] = value[low].astype(BF16)
            out[high] = (value[high] + passed).astype(BF16)
        ring(half, stage, 1 if way == 0 else -1, out, into, sem)

    def far2(half, index):
        value = mixed(half, order[index], 2)
        send_far(
            half, 1, value, far2_out.at[half, index], far2_in.at[half, index],
            lambda way: far2_recv.at[half, index, way],
        )

    def near2(half, index):
        for way, second in ((0, 1), (1, -1)):
            value = mixed(half, order[index], second)
            send_near(
                half, 1, way, value, far2_in.at[half, index, way], far2_recv.at[half, index, way],
                near2_out.at[half, index, way], near2_in.at[half, index, way], near2_recv.at[half, index, way],
            )

    def total2(half, index):
        value = mixed(half, order[index], 0)
        for way in range(2):
            arrive(near2_in.at[half, index, way], near2_recv.at[half, index, way])
            value = value + near2_in[half, index, way].astype(F32)
        return value

    def stage1(half, index):
        value = total2(half, index)
        first = order[index]
        if first == 2:
            send_far(
                half, 0, value, far1_out.at[half], far1_in.at[half], lambda way: far1_recv.at[half, way]
            )
        elif first != 0:
            way = 0 if first == 1 else 1
            send_near(
                half, 0, way, value, far1_in.at[half, way], far1_recv.at[half, way],
                near1_out.at[half, way], near1_in.at[half, way], near1_recv.at[half, way],
            )
        else:
            for way in range(2):
                arrive(near1_in.at[half, way], near1_recv.at[half, way])
                value = value + near1_in[half, way].astype(F32)
            side_out[half] = value.astype(BF16)
            pltpu.make_async_remote_copy(
                src_ref=side_out.at[half], dst_ref=side_in.at[half],
                send_sem=side_send, recv_sem=side_recv.at[half],
                device_id=other_side, device_id_type=MESH,
            ).start()

    for half in both:
        far2(half, 0)
    for index in range(4):
        if index < 3:
            for half in both:
                far2(half, index + 1)
        for half in both:
            near2(half, index)
        if index > 0:
            for half in both:
                stage1(half, index - 1)
    for half in both:
        stage1(half, 3)
    for half in both:
        arrive(side_in.at[half], side_recv.at[half])
        moe_ref[:, half * HALF : (half + 1) * HALF] = (
            side_out[half].astype(F32) + side_in[half].astype(F32)
        ).astype(BF16)

    came = out_ref_in.at[pl.ds(0, 3)]
    pltpu.make_async_copy(came, came, land_send).wait()
    for ref in (far2_out, near2_out, far1_out, near1_out):
        pltpu.make_async_copy(ref, ref, ring_send).wait()
    pltpu.make_async_copy(side_out, side_out, side_send).wait()


def combine(expert_out, weight):
    vmem = pl.BlockSpec(memory_space=pltpu.VMEM)
    dma = pltpu.SemaphoreType.DMA
    return pl.pallas_call(
        combine_kernel,
        out_shape=jax.ShapeDtypeStruct((ROWS, D), BF16),
        in_specs=[vmem] * 2,
        out_specs=vmem,
        scratch_shapes=[
            pltpu.VMEM((2, BLOCKS, 3, SLOTS, HALF), BF16),
            pltpu.VMEM((2, 4, ROWS, HALF), BF16),
            pltpu.VMEM((2, 4, 2, ROWS, HALF), BF16),
            pltpu.VMEM((2, 4, 2, ROWS // 2, HALF), BF16),
            pltpu.VMEM((2, 4, 2, ROWS, HALF), BF16),
            pltpu.VMEM((2, ROWS, HALF), BF16),
            pltpu.VMEM((2, 2, ROWS, HALF), BF16),
            pltpu.VMEM((2, 2, ROWS // 2, HALF), BF16),
            pltpu.VMEM((2, 2, ROWS, HALF), BF16),
            pltpu.VMEM((2, ROWS, HALF), BF16),
            pltpu.VMEM((2, ROWS, HALF), BF16),
            dma, dma((2, BLOCKS)), dma, dma((2, 4, 2)), dma((2, 4, 2)), dma((2, 2)), dma((2, 2)), dma, dma((2,)),
        ],
        compiler_params=pltpu.CompilerParams(
            collective_id=1, has_side_effects=True, vmem_limit_bytes=48 * 1024 * 1024
        ),
        name="combine",
    )(expert_out, weight)


def attend_local(queries, cache_keys, cache_values, new_key, new_value, cache_lengths):
    row_count = queries.shape[0]
    cache_len = cache_keys.shape[1]
    groups = cache_keys.shape[2] // HEAD_DIM
    per_group = HEADS // KV_HEADS
    score_scale = HEAD_DIM ** (-0.5)
    query_heads = queries.reshape(row_count, groups, per_group, HEAD_DIM)
    key_heads = cache_keys.reshape(row_count, cache_len, groups, HEAD_DIM)
    value_heads = cache_values.reshape(row_count, cache_len, groups, HEAD_DIM)
    scores = (
        jnp.einsum("tgqd,tlgd->tgql", query_heads, key_heads, preferred_element_type=jnp.float32)
        * score_scale
    )
    own_key = new_key.reshape(row_count, groups, HEAD_DIM)
    own_score = (
        jnp.einsum("tgqd,tgd->tgq", query_heads, own_key, preferred_element_type=jnp.float32)
        * score_scale
    )
    visible = jnp.arange(cache_len, dtype=jnp.int32)[None, :] < cache_lengths[:, None]
    scores = jnp.where(visible[:, None, None, :], scores, -1e30)
    top_score = jnp.maximum(jnp.max(scores, axis=3), own_score)
    exp_scores = jnp.exp(scores - top_score[..., None])
    own_exp = jnp.exp(own_score - top_score)
    denominator = jnp.sum(exp_scores, axis=3) + own_exp
    attn_weights = (exp_scores / denominator[..., None]).astype(jnp.bfloat16)
    own_prob = (own_exp / denominator).astype(jnp.bfloat16)
    combined = jnp.einsum(
        "tgql,tlgd->tgqd", attn_weights, value_heads, preferred_element_type=jnp.float32
    )
    own_value = new_value.reshape(row_count, groups, 1, HEAD_DIM).astype(jnp.float32)
    combined = combined + own_prob.astype(jnp.float32)[..., None] * own_value
    return combined.reshape(row_count, groups * per_group * HEAD_DIM).astype(jnp.bfloat16)


def per_device(
    queries,
    cache_keys,
    cache_values,
    new_key,
    new_value,
    cache_lengths,
    hidden,
    norm_gain,
    expert_ids,
    router_probs,
    w_gate,
    w_up,
    w_down,
):
    context = attend_local(queries, cache_keys, cache_values, new_key, new_value, cache_lengths)
    rows, weight = dispatch(hidden, norm_gain.reshape(1, D), expert_ids, router_probs)
    rows = rows.reshape(GROUPS * BLOCKS * SLOTS, D)
    gate_act = jnp.dot(rows, w_gate[0], preferred_element_type=jnp.float32)
    up_act = jnp.dot(rows, w_up[0], preferred_element_type=jnp.float32)
    activation = (jax.nn.silu(gate_act) * up_act).astype(jnp.bfloat16)
    partial_out = jnp.dot(activation, w_down[0], preferred_element_type=jnp.float32).astype(jnp.bfloat16)
    moe_out = combine(partial_out.reshape(GROUPS, BLOCKS, SLOTS, D), weight)
    return (context, moe_out)


def solution(mesh):
    in_specs = (
        P("dev", "side"),
        P("dev", None, "side"),
        P("dev", None, "side"),
        P("dev", "side"),
        P("dev", "side"),
        P("dev"),
        P("dev", None),
        P(),
        P("dev", None),
        P("dev", None),
        P("dev", None, "side"),
        P("dev", None, "side"),
        P("dev", "side", None),
    )
    out_specs = (P("dev", "side"), P("dev", None))
    return jax.shard_map(
        per_device, mesh=mesh, in_specs=in_specs, out_specs=out_specs, check_vma=False
    )
```

time: 174 us -> 125 us (0.72)
  Pallas kernels: 0 us -> 87.6 us
  blocking collectives: 84.2 us -> 0 us
  waiting for transfers between devices: 47.8 us -> 0 us
  starting transfers between devices: 5.68 us -> 0 us
  other arithmetic: 5.51 us -> 1.26 us
  local copies, waits for them, and re-layouts: 6.81 us -> 10.5 us
  matrix products: 22.4 us -> 24.7 us
    pallas_call x0 -> x2, Pallas kernels: none -> 87.6 us  [the longest x1 46 us: combine(): pl.pallas_call(combine_kernel, out_shape=jax.ShapeDtypeStruct((ROWS, D),...]
    all_to_all x1 -> x0, blocking collectives: 61.6 us -> none  [per_device(): lax.all_to_all(buffer, 'dev', split_axis=0, concat_axis=0, tiled=True)]
    all_to_all x1 -> x0, waiting for transfers between devices: 47.8 us -> none  [per_device(): lax.all_to_all(partial_out, 'dev', split_axis=0, concat_axis=0, tiled=True)]
    psum x1 -> x0, blocking collectives: 22.6 us -> none  [per_device(): combined = lax.psum(local_mix, 'side')]
    unnamed x25 -> x17, local copies, waits for them, and re-layouts: 1.68 us -> 8.32 us
    all_to_all x1 -> x0, starting transfers between devices: 5.68 us -> none  [per_device(): lax.all_to_all(partial_out, 'dev', split_axis=0, concat_axis=0, tiled=True)]
    convert_element_type x2 -> x0, local copies, waits for them, and re-layouts: 4.42 us -> none  [the longest x1 4.27 us: per_device(): partial_out = jnp.einsum('scf,fd->scd', activation, w_down[0], preferred_...]
    reduce_sum x4 -> x0, other arithmetic: 2.64 us -> none  [the longest x1 1.11 us: per_device(): jnp.mean(hidden_wide * hidden_wide, axis=1, keepdims=True) + 1e-06]
  transfers between devices with their start and end apart: 1 -> 0, of which waited for: 1 -> 0; matrix products, arithmetic and copies ran while one was open for 4% -> 0% of each run, Pallas kernels for 0% -> 0%
where the time goes in v1:
time: 125 us
  Pallas kernels  87.6 us (70%)
  matrix products  24.7 us (20%)
  local copies, waits for them, and re-layouts  10.5 us (8%)
  other arithmetic  1.26 us (1%)
    pallas_call x1, Pallas kernels, combine(): pl.pallas_call(combine_kernel, out_shape=jax.ShapeDtypeStruct((ROWS, D),...  46 us
    pallas_call x1, Pallas kernels, dispatch(): pl.pallas_call(dispatch_kernel, out_shape=(jax.ShapeDtypeStruct((GROUPS,...  41.5 us
    dot_general x1, matrix products, per_device(): jnp.dot(activation, w_down[0], preferred_element_type=jnp.float32)  16.6 us
    unnamed x17, local copies, waits for them, and re-layouts  8.32 us
    dot_general x1, matrix products, attend_local(): jnp.einsum('tgqd,tlgd->tgql', query_heads, key_heads, preferred_element_t...  3.5 us
    dot_general x1, matrix products, per_device(): gate_act = jnp.dot(rows, w_gate[0], preferred_element_type=jnp.float32)  3.4 us

profile of v1, /device:TPU:2, one launch (start us, length us, event | category | flops | bytes accessed | tf_op | source)
XLA Modules:
  0.0 124.7 jit_solution(114496222845488131)
XLA Ops:
  0.6 0.7 iota_compare_fusion
  1.4 0.7 reshape.61.gain_ref
  2.1 0.8 copy.17.ids_ref
  2.8 0.8 copy.18.probs_ref
  3.6 0.7 reshape.68
  4.3 0.7 reshape.64
  5.1 0.0 copy-start.3
  5.1 1.1 copy.23
  6.2 0.2 fusion.38
  6.5 3.5 %fusion.37 = (f32[32,2,16]{2,1,0:T(2,128)S(1)}, f32[32,2,16,256]{3,2,1,0:T(8,128)S(1)}) fusion(bf16[32,2,16,128]{3,2,1,0:T(8,128)(2,1)S(1)} %bitcast.60, pred[32,256]{1,0:T(8,128)(4,1)S(1)} %iota_compare_fusion, bf16[32,256,256]{2,1,0:T(8,128)(2,1)} %param.14), kind=kOutput, calls=%fused_computation.31 | convolution fusion | flops 67894272 | bytes 5517312 | tf_op jit(solution)/shard_map/tgqd,tlgd->tgql/dot_general | solution.py:465
  10.0 0.0 slice-start
  10.0 0.4 fusion.29
  10.5 0.1 fusion.34
  10.5 0.0 copy-start.1
  10.6 0.0 slice-start.1
  10.6 0.9 fusion.26
  11.5 0.8 copy.44
  12.3 41.5 %dispatch.1 = (bf16[4,16,8,4096]{3,2,1,0:T(8,128)(2,1)S(1)}, f32[16,32,32]{2,1,0:T(8,128)S(1)}) custom-call(bf16[32,4096]{1,0:T(8,128)(2,1)S(1)} %copy-done.1, bf16[1,4096]{1,0:T(2,128)(2,1)S(1)} %reshape.61.gain_ref, s32[32,8]{1,0:T(8,128)S(1)} %copy.17.ids_ref, f32[32,8]{1,0:T(8,128)S(1)} %copy.18.probs_ref), custom_call_target="tpu_custom_call" | custom-call | tf_op jit(solution)/shard_map/dispatch/pallas_call | solution.py:252
  53.9 1.9 %copy-done.2 = bf16[4,16,8,4096]{3,2,1,0:T(8,128)(2,1)} copy-done((bf16[4,16,8,4096]{3,2,1,0:T(8,128)(2,1)}, bf16[4,16,8,4096]{3,2,1,0:T(8,128)(2,1)S(1)}, u32[]{:S(2)}) %copy-start.2) | copy-done | bytes 4194328
  55.8 3.4 %fusion.4 = f32[512,768]{1,0:T(8,128)S(1)} fusion(bf16[512,4096]{1,0:T(8,128)(2,1)S(1)} %bitcast.57, bf16[1,4096,768]{2,1,0:T(8,128)(2,1)S(1)} %bitcast.67), kind=kOutput, calls=%fused_computation.4 | convolution fusion | flops 3221225472 | bytes 12058624 | tf_op jit(solution)/shard_map/dot_general | solution.py:507
  59.2 16.6 %fusion.6 = bf16[512,4096]{1,0:T(8,128)(2,1)} fusion(bf16[1,768,4096]{2,1,0:T(8,128)(2,1)} %param.25, f32[512,768]{1,0:T(8,128)S(1)} %fusion.4, bf16[512,4096]{1,0:T(8,128)(2,1)} %bitcast.58, bf16[1,4096,768]{2,1,0:T(8,128)(2,1)} %param.24), kind=kOutput, calls=%fused_computation.6 | convolution fusion | flops 6446907392 | bytes 22544384 | tf_op jit(solution)/shard_map/dot_general | solution.py:510
  75.8 2.2 %copy-done = bf16[512,4096]{1,0:T(8,128)(2,1)S(1)} copy-done((bf16[512,4096]{1,0:T(8,128)(2,1)S(1)}, bf16[512,4096]{1,0:T(8,128)(2,1)}, u32[]{:S(2)}) %copy-start) | copy-done | bytes 4194328
  78.0 46.0 %combine.1 = bf16[32,4096]{1,0:T(8,128)(2,1)S(1)} custom-call(bf16[4,16,8,4096]{3,2,1,0:T(8,128)(2,1)S(1)} %bitcast.56, f32[16,32,32]{2,1,0:T(8,128)S(1)} %get-tuple-element.5.weight_ref), custom_call_target="tpu_custom_call" | custom-call | tf_op jit(solution)/shard_map/combine/pallas_call | solution.py:429
  124.0 0.7 copy.46
  (8 shorter events, 0.0 us)
Async XLA Ops:
  5.1 5.5 %copy-start.3 = (bf16[32,256,256]{2,1,0:T(8,128)(2,1)S(1)}, bf16[32,256,256]{2,1,0:T(8,128)(2,1)}, u32[]{:S(2)}) copy-start(bf16[32,256,256]{2,1,0:T(8,128)(2,1)} %param.15) | copy-start | bytes 12582916
  10.0 45.8 %slice-start = ((s8[6291456]{0:T(1024)(128)(4,1)}), s8[4194304]{0:T(1024)(128)(4,1)S(1)}, s32[]{:S(2)}) async-start(s8[6291456]{0:T(1024)(128)(4,1)} %bitcast.66), calls=%async_computation | async-start | bytes 8388608
  10.5 1.8 %copy-start.1 = (bf16[32,4096]{1,0:T(8,128)(2,1)S(1)}, bf16[32,4096]{1,0:T(8,128)(2,1)}, u32[]{:S(2)}) copy-start(bf16[32,4096]{1,0:T(8,128)(2,1)} %hidden_ref.1) | copy-start | bytes 786436
  10.6 45.3 %slice-start.1 = ((s8[6291456]{0:T(1024)(128)(4,1)}), s8[2097152]{0:T(1024)(128)(4,1)S(1)}, s32[]{:S(2)}) async-start(s8[6291456]{0:T(1024)(128)(4,1)} %bitcast.66), calls=%async_computation.1 | async-start | bytes 4194304
  53.9 1.9 %copy-start.2 = (bf16[4,16,8,4096]{3,2,1,0:T(8,128)(2,1)}, bf16[4,16,8,4096]{3,2,1,0:T(8,128)(2,1)S(1)}, u32[]{:S(2)}) copy-start(bf16[4,16,8,4096]{3,2,1,0:T(8,128)(2,1)S(1)} %get-tuple-element.4) | copy-start | bytes 12582916
  75.8 2.2 %copy-start = (bf16[512,4096]{1,0:T(8,128)(2,1)S(1)}, bf16[512,4096]{1,0:T(8,128)(2,1)}, u32[]{:S(2)}) copy-start(bf16[512,4096]{1,0:T(8,128)(2,1)} %fusion.6) | copy-start | bytes 12582916

commit v2 on v1

v2 whole, which is shorter than its diff:
```python
import functools

import jax
import jax.numpy as jnp
from jax import lax
from jax.experimental import pallas as pl
from jax.experimental.pallas import tpu as pltpu
from jax.sharding import PartitionSpec as P

HEADS = 64
KV_HEADS = 4
HEAD_DIM = 128
RING = 4
BLOCKS = 16
ROWS = 32
SLOTS = 8
GROUPS = 4
D = 4096
HALF = 2048
TAIL = 128
WIDE = HALF + TAIL
MESH = pl.DeviceIdType.MESH
F32 = jnp.float32
BF16 = jnp.bfloat16


class Place:
    def __init__(self):
        self.side = lax.axis_index("side")
        dev = lax.axis_index("dev")
        self.dev = dev
        self.core = dev % 2
        self.x = (dev // 2) % RING
        self.z = (dev // 8) % RING
        self.lo = dev // 32
        self.y = self.side * 2 + self.lo

    @staticmethod
    def index(lo, z, x, core):
        return ((lo * RING + z) * RING + x) * 2 + core

    def plane(self, axis, step):
        if axis == "x":
            return (self.side, self.index(self.lo, self.z, (self.x + step) % RING, self.core))
        return (self.side, self.index(self.lo, (self.z + step) % RING, self.x, self.core))

    def along_y(self, step, core):
        y = (self.y + step) % RING
        return (y // 2, self.index(y % 2, self.z, self.x, core))

    def sibling(self):
        return (self.side, self.index(self.lo, self.z, self.x, 1 - self.core))

    def block(self, half, first, second):
        if half == 0:
            x, z = (self.x + first) % RING, (self.z + second) % RING
        else:
            z, x = (self.z + first) % RING, (self.x + second) % RING
        return z * RING + x


AXES = (("x", "z"), ("z", "x"))
NEAR = (0, -1, 1, 2)


def routing_table(ids_ref, probs_ref):
    lane = lax.broadcasted_iota(jnp.int32, (ROWS, TAIL), 1)
    expert = lane % 64
    ids = ids_ref[...]
    probs = probs_ref[...]
    share = probs / jnp.sum(probs, axis=1, keepdims=True)
    hit = jnp.zeros((ROWS, TAIL), F32)
    gate = jnp.zeros((ROWS, TAIL), F32)
    for k in range(ids.shape[1]):
        match = ids[:, k : k + 1] == expert
        hit = jnp.where(match, 1.0, hit)
        gate = jnp.where(match, share[:, k : k + 1], gate)
    row = lax.broadcasted_iota(jnp.int32, (ROWS, ROWS), 0)
    col = lax.broadcasted_iota(jnp.int32, (ROWS, ROWS), 1)
    before = jnp.where(col < row, 1.0, 0.0).astype(BF16)
    rank = jnp.dot(before, hit.astype(BF16), preferred_element_type=F32)
    rank = jnp.where(hit > 0.5, rank, 100.0)
    lead = gate.astype(BF16)
    trail = (gate - lead.astype(F32)).astype(BF16)
    left = lane < 64
    rank = rank.astype(BF16)
    return jnp.where(left, rank, lead), jnp.where(left, rank, trail)


CHUNK = 4
KEYS = 256
HIDDEN = 768


def step_kernel(
    hidden_ref, gain_ref, ids_ref, probs_ref, lengths_ref, queries_ref, new_key_ref, new_value_ref,
    keys_hbm, values_hbm, w_gate_hbm, w_up_hbm, w_down_hbm,
    context_ref, moe_ref,
    gathered, picked_y, picked_s, rows_in, weights, w_gate, w_up, w_down, active, rows_out,
    landed, far2_out, near2_out, far2_in, near2_in, far1_out, near1_out, far1_in, near1_in,
    side_out, side_in, keys, values,
    ag_send, ag_recv, pick_send, rows_recv, w_sem, kv_sem,
    land_send, land_recv, ring_send, far2_recv, near2_recv, far1_recv, near1_recv, side_send, side_recv,
):
    me = Place()
    both = range(2)
    lo = 1 - me.lo
    own_group = me.lo * 2 + me.core
    other_side = (1 - me.side, me.dev)

    w_copies = [
        pltpu.make_async_copy(w_gate_hbm, w_gate, w_sem.at[0]),
        pltpu.make_async_copy(w_up_hbm, w_up, w_sem.at[1]),
        pltpu.make_async_copy(w_down_hbm, w_down, w_sem.at[2]),
    ]

    def cache_copies(chunk):
        tokens = pl.ds(chunk * CHUNK, CHUNK)
        slot = chunk % 2
        return (
            pltpu.make_async_copy(keys_hbm.at[tokens], keys.at[slot], kv_sem.at[slot, 0]),
            pltpu.make_async_copy(values_hbm.at[tokens], values.at[slot], kv_sem.at[slot, 1]),
        )

    for chunk in range(2):
        for copy in cache_copies(chunk):
            copy.start()
    for copy in w_copies:
        copy.start()

    neighbours = (
        [me.plane(axis, step) for axis in ("x", "z") for step in (-1, 1)]
        + [me.along_y(step, core) for step in (-1, 1) for core in (0, 1)]
        + [me.sibling(), other_side]
    )
    barrier = pltpu.get_barrier_semaphore()
    for device in neighbours:
        pl.semaphore_signal(barrier, inc=1, device_id=device, device_id_type=MESH)

    wide = hidden_ref[...].astype(F32)
    inverse = lax.rsqrt(jnp.mean(wide * wide, axis=1, keepdims=True) + 1e-06)
    normed = (wide * inverse * gain_ref[...].astype(F32)).astype(BF16)
    tables = routing_table(ids_ref, probs_ref)
    own_block = me.block(0, 0, 0)
    for half in both:
        gathered[half, own_block, :, 0:HALF] = normed[:, half * HALF : (half + 1) * HALF]
        gathered[half, own_block, :, HALF:WIDE] = tables[half]

    experts = (
        me.dev,
        me.index(me.lo, me.z, me.x, 1 - me.core),
        me.index(lo, me.z, me.x, 0),
        me.index(lo, me.z, me.x, 1),
    )
    slot_of = lax.broadcasted_iota(jnp.int32, (GROUPS * SLOTS, TAIL), 0)
    lane = lax.broadcasted_iota(jnp.int32, (GROUPS * SLOTS, TAIL), 1)
    wanted = jnp.zeros((GROUPS * SLOTS, TAIL), jnp.int32)
    for j in range(GROUPS):
        wanted = jnp.where(slot_of // SLOTS == j, experts[j], wanted)
    pick_rank = jnp.where(lane == wanted, 1.0, 0.0).astype(BF16)
    pick_gate = jnp.where(lane == wanted + 64, 1.0, 0.0).astype(BF16)

    pl.semaphore_wait(barrier, len(neighbours))

    def hop(half, block, rows, stage, step, sem):
        ref = gathered.at[half, block, rows]
        return pltpu.make_async_remote_copy(
            src_ref=ref, dst_ref=ref, send_sem=ag_send, recv_sem=ag_recv.at[half, sem],
            device_id=me.plane(AXES[half][stage], step), device_id_type=MESH,
        )

    full, low_rows, high_rows = pl.ds(0, ROWS), pl.ds(0, ROWS // 2), pl.ds(ROWS // 2, ROWS // 2)

    def send_both(half, first, stage, base):
        block = me.block(half, first, 0)
        hop(half, block, full, stage, 1, base).start()
        hop(half, block, full, stage, -1, base + 1).start()

    def landing(ref, sem):
        pltpu.make_async_copy(ref, ref, sem).wait()

    def take_full(half, first, stage, base):
        for step, rows, sem in ((-1, low_rows, base), (1, high_rows, base + 1)):
            block = me.block(half, step, 0) if stage == 0 else me.block(half, first, step)
            landing(gathered.at[half, block], ag_recv.at[half, sem])
            hop(half, block, rows, stage, -step, sem + 2).start()

    def take_far(half, first, stage, base):
        block = me.block(half, 2, 0) if stage == 0 else me.block(half, first, 2)
        landing(gathered.at[half, block, low_rows], ag_recv.at[half, base + 2])
        landing(gathered.at[half, block, high_rows], ag_recv.at[half, base + 3])

    def select(half, first, second):
        block = me.block(half, first, second)
        table = gathered[half, block, :, HALF:WIDE]
        rank = lax.dot_general(pick_rank, table, (((1,), (1,)), ((), ())), preferred_element_type=F32)
        slot = (lax.broadcasted_iota(jnp.int32, (GROUPS * SLOTS, ROWS), 0) % SLOTS).astype(F32)
        hot = jnp.where(rank == slot, 1.0, 0.0).astype(BF16)
        chosen = jnp.dot(hot, gathered[half, block, :, 0:HALF], preferred_element_type=F32).astype(BF16)
        columns = pl.ds(half * HALF, HALF)
        for core in range(2):
            picked_y[half, block, core] = chosen[16 + 8 * core : 24 + 8 * core]
            pltpu.make_async_remote_copy(
                src_ref=picked_y.at[half, block, core],
                dst_ref=rows_in.at[own_group, block, :, columns],
                send_sem=pick_send, recv_sem=rows_recv,
                device_id=me.along_y(1 if half == 0 else -1, core), device_id_type=MESH,
            ).start()
        picked_s[half, block] = chosen[8:16]
        pltpu.make_async_remote_copy(
            src_ref=picked_s.at[half, block],
            dst_ref=rows_in.at[own_group, block, :, columns],
            send_sem=pick_send, recv_sem=rows_recv,
            device_id=me.sibling(), device_id_type=MESH,
        ).start()
        rows_in[own_group, block, :, columns] = chosen[0:8]

    def attend(chunk):
        slot = chunk % 2
        for copy in cache_copies(chunk):
            copy.wait()
        scale = HEAD_DIM ** (-0.5)
        position = lax.broadcasted_iota(jnp.int32, (16, KEYS), 1)
        for item in range(CHUNK):
            token = chunk * CHUNK + item
            visible = position < lengths_ref[token]
            for group in range(2):
                heads = slice(group * 16, (group + 1) * 16)
                lanes = slice(group * HEAD_DIM, (group + 1) * HEAD_DIM)
                query = queries_ref[token, heads]
                scores = lax.dot_general(
                    query, keys[slot, item, :, lanes], (((1,), (1,)), ((), ())), preferred_element_type=F32
                )
                scores = jnp.where(visible, scores * scale, -1e30)
                own_key = new_key_ref[token : token + 1, lanes].astype(F32)
                own = jnp.sum(query.astype(F32) * own_key, axis=1, keepdims=True) * scale
                top = jnp.maximum(jnp.max(scores, axis=1, keepdims=True), own)
                scores = jnp.exp(scores - top)
                own = jnp.exp(own - top)
                total = jnp.sum(scores, axis=1, keepdims=True) + own
                probs = (scores / total).astype(BF16)
                own = (own / total).astype(BF16).astype(F32)
                mixed = jnp.dot(probs, values[slot, item, :, lanes], preferred_element_type=F32)
                mixed = mixed + own * new_value_ref[token : token + 1, lanes].astype(F32)
                context_ref[token, heads] = mixed.astype(BF16)
        if chunk + 2 < ROWS // CHUNK:
            for copy in cache_copies(chunk + 2):
                copy.start()

    for half in both:
        send_both(half, 0, 0, 0)
    for half in both:
        send_both(half, 0, 1, 4)
    for half in both:
        select(half, 0, 0)
    attend(0)
    for half in both:
        take_full(half, 0, 0, 0)
        send_both(half, -1, 1, 8)
    for half in both:
        select(half, -1, 0)
        select(half, 1, 0)
    attend(1)
    for half in both:
        take_full(half, 0, 1, 4)
        send_both(half, 1, 1, 12)
    for half in both:
        take_far(half, 0, 0, 0)
    for half in both:
        select(half, 2, 0)
        select(half, 0, -1)
        select(half, 0, 1)
    attend(2)
    for index in range(1, 4):
        first = NEAR[index]
        for half in both:
            take_full(half, first, 1, 4 + 4 * index)
            if index == 1:
                send_both(half, 2, 1, 16)
        for half in both:
            take_far(half, NEAR[index - 1], 1, 4 * index)
        for half in both:
            select(half, first, -1)
            select(half, first, 1)
            select(half, NEAR[index - 1], 2)
        attend(2 + index)
    for half in both:
        take_far(half, 2, 1, 16)
        select(half, 2, 2)
    attend(6)

    for block in range(BLOCKS):
        rank = lax.dot_general(
            gathered[0, block, :, HALF:WIDE], pick_rank, (((1,), (1,)), ((), ())), preferred_element_type=F32
        )
        gate = sum(
            lax.dot_general(
                gathered[half, block, :, HALF:WIDE], pick_gate, (((1,), (1,)), ((), ())), preferred_element_type=F32
            )
            for half in both
        )
        slot = (lax.broadcasted_iota(jnp.int32, (ROWS, GROUPS * SLOTS), 1) % SLOTS).astype(F32)
        weights[block] = jnp.where(rank == slot, gate, 0.0)
    attend(7)

    for copy in w_copies:
        copy.wait()
    landing(rows_in.at[pl.ds(0, 3)], rows_recv)

    def expert(base):
        rows = rows_in[pl.ds(base, 2)].reshape(2 * BLOCKS * SLOTS, D)
        for low in range(0, HIDDEN, 256):
            columns = slice(low, low + 256)
            gate = jnp.dot(rows, w_gate[:, columns], preferred_element_type=F32)
            up = jnp.dot(rows, w_up[:, columns], preferred_element_type=F32)
            active[:, columns] = (gate / (1.0 + jnp.exp(-gate)) * up).astype(BF16)

    def expert_down(base, half):
        for low in range(half * HALF, (half + 1) * HALF, 512):
            columns = slice(low, low + 512)
            out = jnp.dot(active[...], w_down[:, columns], preferred_element_type=F32).astype(BF16)
            rows_out[pl.ds(base, 2), :, :, columns] = out.reshape(2, BLOCKS, SLOTS, 512)

    far_order = (2, 1, -1, 0)
    visits = (
        (2, 2), (1, 2), (2, 1), (2, -1), (-1, 2), (1, 1), (1, -1), (2, 0),
        (0, 2), (-1, 1), (-1, -1), (1, 0), (0, 1), (0, -1), (-1, 0), (0, 0),
    )

    def give_y(half, visit):
        block = me.block(half, *visits[visit])
        columns = pl.ds(half * HALF, HALF)
        for core in range(2):
            pltpu.make_async_remote_copy(
                src_ref=rows_out.at[lo * 2 + core, block, :, columns],
                dst_ref=landed.at[half, block, 1 + me.core],
                send_sem=land_send, recv_sem=land_recv.at[half, block],
                device_id=me.along_y(1 if half == 0 else -1, core), device_id_type=MESH,
            ).start()

    def give_sibling(half, visit):
        block = me.block(half, *visits[visit])
        pltpu.make_async_remote_copy(
            src_ref=rows_out.at[me.lo * 2 + 1 - me.core, block, :, pl.ds(half * HALF, HALF)],
            dst_ref=landed.at[half, block, 0],
            send_sem=land_send, recv_sem=land_recv.at[half, block],
            device_id=me.sibling(), device_id_type=MESH,
        ).start()

    AHEAD = 4
    expert(lo * 2)
    for half in both:
        expert_down(lo * 2, half)
        for visit in range(AHEAD):
            give_y(half, visit)
    expert(me.lo * 2)
    for half in both:
        expert_down(me.lo * 2, half)
        for visit in range(AHEAD):
            give_sibling(half, visit)

    turn = [0, 0]

    def mixed(half, first, second):
        assert visits[turn[half]] == (first, second)
        if turn[half] + AHEAD < BLOCKS:
            give_y(half, turn[half] + AHEAD)
            give_sibling(half, turn[half] + AHEAD)
        turn[half] += 1
        block = me.block(half, first, second)
        landing(landed.at[half, block], land_recv.at[half, block])
        weight = weights[block]
        lead = weight.astype(BF16)
        trail = (weight - lead.astype(F32)).astype(BF16)
        own = rows_out[own_group, block, :, pl.ds(half * HALF, HALF)]
        parts = landed[half, block]
        rows = jnp.concatenate([own, parts[0], parts[1], parts[2]], axis=0)
        return jnp.dot(lead, rows, preferred_element_type=F32) + jnp.dot(trail, rows, preferred_element_type=F32)

    def ring(half, stage, step, src, dst, sem):
        pltpu.make_async_remote_copy(
            src_ref=src, dst_ref=dst, send_sem=ring_send, recv_sem=sem,
            device_id=me.plane(AXES[half][stage], step), device_id_type=MESH,
        ).start()

    low, high = slice(0, ROWS // 2), slice(ROWS // 2, ROWS)

    def send_far(half, stage, value, out, into, sems):
        out[...] = value.astype(BF16)
        for way, step, rows in ((0, 1, low_rows), (1, -1, high_rows)):
            ring(half, stage, step, out.at[rows], into.at[way], sems(way))

    def send_near(half, stage, way, value, far_in, far_sem, out, into, sem):
        landing(far_in, far_sem)
        passed = far_in[...].astype(F32)
        if way == 0:
            out[low] = (value[low] + passed).astype(BF16)
            out[high] = value[high].astype(BF16)
        else:
            out[low] = value[low].astype(BF16)
            out[high] = (value[high] + passed).astype(BF16)
        ring(half, stage, 1 if way == 0 else -1, out, into, sem)

    def far2(half, index):
        value = mixed(half, far_order[index], 2)
        send_far(
            half, 1, value, far2_out.at[half, index], far2_in.at[half, index],
            lambda way: far2_recv.at[half, index, way],
        )

    def near2(half, index):
        for way, second in ((0, 1), (1, -1)):
            value = mixed(half, far_order[index], second)
            send_near(
                half, 1, way, value, far2_in.at[half, index, way], far2_recv.at[half, index, way],
                near2_out.at[half, index, way], near2_in.at[half, index, way], near2_recv.at[half, index, way],
            )

    def stage1(half, index):
        value = mixed(half, far_order[index], 0)
        for way in both:
            landing(near2_in.at[half, index, way], near2_recv.at[half, index, way])
            value = value + near2_in[half, index, way].astype(F32)
        first = far_order[index]
        if first == 2:
            send_far(half, 0, value, far1_out.at[half], far1_in.at[half], lambda way: far1_recv.at[half, way])
        elif first != 0:
            way = 0 if first == 1 else 1
            send_near(
                half, 0, way, value, far1_in.at[half, way], far1_recv.at[half, way],
                near1_out.at[half, way], near1_in.at[half, way], near1_recv.at[half, way],
            )
        else:
            for way in both:
                landing(near1_in.at[half, way], near1_recv.at[half, way])
                value = value + near1_in[half, way].astype(F32)
            side_out[half] = value.astype(BF16)
            pltpu.make_async_remote_copy(
                src_ref=side_out.at[half], dst_ref=side_in.at[half],
                send_sem=side_send, recv_sem=side_recv.at[half],
                device_id=other_side, device_id_type=MESH,
            ).start()

    for half in both:
        far2(half, 0)
    for index in range(4):
        if index < 3:
            for half in both:
                far2(half, index + 1)
        for half in both:
            near2(half, index)
        if index > 0:
            for half in both:
                stage1(half, index - 1)
    for half in both:
        stage1(half, 3)
    for half in both:
        landing(side_in.at[half], side_recv.at[half])
        moe_ref[:, half * HALF : (half + 1) * HALF] = (
            side_out[half].astype(F32) + side_in[half].astype(F32)
        ).astype(BF16)

    landing(gathered.at[:, pl.ds(0, 15)], ag_send)
    landing(picked_y, pick_send)
    landing(picked_s, pick_send)
    landing(rows_out.at[pl.ds(0, 3)], land_send)
    for ref in (far2_out, near2_out, far1_out, near1_out):
        landing(ref, ring_send)
    landing(side_out, side_send)


def per_device(
    queries,
    cache_keys,
    cache_values,
    new_key,
    new_value,
    cache_lengths,
    hidden,
    norm_gain,
    expert_ids,
    router_probs,
    w_gate,
    w_up,
    w_down,
):
    vmem = pl.BlockSpec(memory_space=pltpu.VMEM)
    smem = pl.BlockSpec(memory_space=pltpu.SMEM)
    hbm = pl.BlockSpec(memory_space=pl.ANY)
    dma = pltpu.SemaphoreType.DMA

    def bf16(*shape):
        return pltpu.VMEM(shape, BF16)

    context, moe_out = pl.pallas_call(
        step_kernel,
        out_shape=(
            jax.ShapeDtypeStruct((ROWS, 32, HEAD_DIM), BF16),
            jax.ShapeDtypeStruct((ROWS, D), BF16),
        ),
        in_specs=[vmem] * 4 + [smem] + [vmem] * 3 + [hbm] * 5,
        out_specs=(vmem, vmem),
        scratch_shapes=[
            bf16(2, BLOCKS, ROWS, WIDE),
            bf16(2, BLOCKS, 2, SLOTS, HALF),
            bf16(2, BLOCKS, SLOTS, HALF),
            bf16(GROUPS, BLOCKS, SLOTS, D),
            pltpu.VMEM((BLOCKS, ROWS, GROUPS * SLOTS), F32),
            bf16(D, HIDDEN),
            bf16(D, HIDDEN),
            bf16(HIDDEN, D),
            bf16(2 * BLOCKS * SLOTS, HIDDEN),
            bf16(GROUPS, BLOCKS, SLOTS, D),
            bf16(2, BLOCKS, 3, SLOTS, HALF),
            bf16(2, 4, ROWS, HALF),
            bf16(2, 4, 2, ROWS, HALF),
            bf16(2, 4, 2, ROWS // 2, HALF),
            bf16(2, 4, 2, ROWS, HALF),
            bf16(2, ROWS, HALF),
            bf16(2, 2, ROWS, HALF),
            bf16(2, 2, ROWS // 2, HALF),
            bf16(2, 2, ROWS, HALF),
            bf16(2, ROWS, HALF),
            bf16(2, ROWS, HALF),
            bf16(2, CHUNK, KEYS, 2 * HEAD_DIM),
            bf16(2, CHUNK, KEYS, 2 * HEAD_DIM),
            dma, dma((2, 20)), dma, dma, dma((3,)), dma((2, 2)),
            dma, dma((2, BLOCKS)), dma, dma((2, 4, 2)), dma((2, 4, 2)), dma((2, 2)), dma((2, 2)), dma, dma((2,)),
        ],
        compiler_params=pltpu.CompilerParams(
            collective_id=0, has_side_effects=True, vmem_limit_bytes=58 * 1024 * 1024
        ),
        name="step",
    )(
        hidden, norm_gain.reshape(1, D), expert_ids, router_probs, cache_lengths,
        queries.reshape(ROWS, 32, HEAD_DIM), new_key, new_value,
        cache_keys, cache_values, w_gate[0], w_up[0], w_down[0],
    )
    return (context.reshape(ROWS, 32 * HEAD_DIM), moe_out)


def solution(mesh):
    in_specs = (
        P("dev", "side"),
        P("dev", None, "side"),
        P("dev", None, "side"),
        P("dev", "side"),
        P("dev", "side"),
        P("dev"),
        P("dev", None),
        P(),
        P("dev", None),
        P("dev", None),
        P("dev", None, "side"),
        P("dev", None, "side"),
        P("dev", "side", None),
    )
    out_specs = (P("dev", "side"), P("dev", None))
    return jax.shard_map(
        per_device, mesh=mesh, in_specs=in_specs, out_specs=out_specs, check_vma=False
    )
```

time: 125 us -> 103 us (0.82)
  matrix products: 24.7 us -> 0 us
  Pallas kernels: 87.6 us -> 92 us
  local copies, waits for them, and re-layouts: 10.5 us -> 9.17 us
  other arithmetic: 1.26 us -> 0 us
    dot_general x5 -> x0, matrix products: 24.7 us -> none  [the longest x1 16.6 us: per_device(): jnp.dot(activation, w_down[0], preferred_element_type=jnp.float32)]
    pallas_call x2 -> x1, Pallas kernels: 87.6 us -> 92 us  [per_device(): pl.pallas_call(step_kernel, out_shape=(jax.ShapeDtypeStruct((ROWS, 32, HE...]
    unnamed x17 -> x5, local copies, waits for them, and re-layouts: 8.32 us -> 7.85 us
where the time goes in v2:
time: 103 us; the launch traced here: 102 us
  Pallas kernels  92 us (89%)
  local copies, waits for them, and re-layouts  9.17 us (9%)
    pallas_call x1, Pallas kernels, per_device(): pl.pallas_call(step_kernel, out_shape=(jax.ShapeDtypeStruct((ROWS, 32, HE...  92 us
    unnamed x5, local copies, waits for them, and re-layouts  7.85 us

profile of v2, /device:TPU:2, one launch (start us, length us, event | category | flops | bytes accessed | tf_op | source)
XLA Modules:
  0.0 101.8 jit_solution(11072790582771207087)
XLA Ops:
  0.6 1.3 %reshape.13.gain_ref = bf16[1,4096]{1,0:T(2,128)(2,1)} reshape(bf16[4096]{0:T(1024)(128)(2,1)} %param.20) | data formatting | bytes 16384 | tf_op jit(solution)/shard_map/reshape | solution.py:535
  1.9 1.4 %copy.15.ids_ref = s32[32,8]{1,0:T(8,128)} copy(s32[32,8]{0,1:T(8,128)} %param.21) | data formatting | bytes 2048 | tf_op args[8]
  3.3 1.4 %copy.16.probs_ref = f32[32,8]{1,0:T(8,128)} copy(f32[32,8]{0,1:T(8,128)} %param.22) | data formatting | bytes 2048 | tf_op args[9]
  4.7 1.7 %copy.17 = bf16[4,8,32,128]{3,2,1,0:T(8,128)(2,1)} copy(bf16[4,8,32,128]{3,1,2,0:T(8,128)(2,1)} %bitcast.13) | data formatting | bytes 524288
  6.4 92.0 %step.1 = (bf16[32,32,128]{2,1,0:T(8,128)(2,1)}, bf16[32,4096]{1,0:T(8,128)(2,1)}) custom-call(bf16[32,4096]{1,0:T(8,128)(2,1)} %hidden_ref.1, bf16[1,4096]{1,0:T(2,128)(2,1)} %reshape.13.gain_ref, s32[32,8]{1,0:T(8,128)} %copy.15.ids_ref, f32[32,8]{1,0:T(8,128)} %copy.16.probs_ref, s32[32]{0:T(128)} %lengths_ref.1, bf16[32,32,128]{2,1,0:T(8,128)(2,1)} %bitcast.12, ...), custom_call_target="tpu_custom_call" | custom-call | tf_op jit(solution)/shard_map/step/pallas_call | solution.py:495
  98.4 1.8 %copy.20 = bf16[4,8,32,128]{3,1,2,0:T(8,128)(2,1)} copy(bf16[4,8,32,128]{3,2,1,0:T(8,128)(2,1)} %bitcast.15) | data formatting | bytes 524288
  100.2 1.7 %copy.22 = bf16[32,4096]{1,0:T(8,128)(2,1)} copy(bf16[32,4096]{1,0:T(8,128)(2,1)} %get-tuple-element.9) | data formatting | bytes 524288

commit v3 on v2

--- a/solution.py
+++ b/solution.py
@@ -64,31 +64,36 @@
 
 
 def routing_table(ids_ref, probs_ref):
-    lane = lax.broadcasted_iota(jnp.int32, (ROWS, TAIL), 1)
-    expert = lane % 64
+    place = lax.broadcasted_iota(jnp.int32, (TAIL, ROWS), 0)
+    expert = place % 64
     ids = ids_ref[...]
     probs = probs_ref[...]
-    share = probs / jnp.sum(probs, axis=1, keepdims=True)
-    hit = jnp.zeros((ROWS, TAIL), F32)
-    gate = jnp.zeros((ROWS, TAIL), F32)
-    for k in range(ids.shape[1]):
-        match = ids[:, k : k + 1] == expert
+    share = probs / jnp.sum(probs, axis=0, keepdims=True)
+    hit = jnp.zeros((TAIL, ROWS), F32)
+    gate = jnp.zeros((TAIL, ROWS), F32)
+    for k in range(ids.shape[0]):
+        match = ids[k : k + 1, :] == expert
         hit = jnp.where(match, 1.0, hit)
-        gate = jnp.where(match, share[:, k : k + 1], gate)
+        gate = jnp.where(match, share[k : k + 1, :], gate)
     row = lax.broadcasted_iota(jnp.int32, (ROWS, ROWS), 0)
     col = lax.broadcasted_iota(jnp.int32, (ROWS, ROWS), 1)
-    before = jnp.where(col < row, 1.0, 0.0).astype(BF16)
-    rank = jnp.dot(before, hit.astype(BF16), preferred_element_type=F32)
+    before = jnp.where(row < col, 1.0, 0.0).astype(BF16)
+    same = jnp.where(row == col, 1.0, 0.0).astype(BF16)
+    rank = jnp.dot(hit.astype(BF16), before, preferred_element_type=F32)
     rank = jnp.where(hit > 0.5, rank, 100.0)
-    lead = gate.astype(BF16)
-    trail = (gate - lead.astype(F32)).astype(BF16)
-    left = lane < 64
-    rank = rank.astype(BF16)
-    return jnp.where(left, rank, lead), jnp.where(left, rank, trail)
+    lead = gate.astype(BF16).astype(F32)
+    first = place < 64
+    return tuple(
+        lax.dot_general(
+            same, jnp.where(first, rank, part).astype(BF16), (((1,), (1,)), ((), ())), preferred_element_type=F32
+        ).astype(BF16)
+        for part in (lead, gate - lead)
+    )
 
 
 CHUNK = 4
 KEYS = 256
+HEADS_HERE = 32
 HIDDEN = 768
 
 
@@ -98,7 +103,7 @@
     context_ref, moe_ref,
     gathered, picked_y, picked_s, rows_in, weights, w_gate, w_up, w_down, active, rows_out,
     landed, far2_out, near2_out, far2_in, near2_in, far1_out, near1_out, far1_in, near1_in,
-    side_out, side_in, keys, values,
+    side_out, side_in, keys, values, query_rows, context_rows,
     ag_send, ag_recv, pick_send, rows_recv, w_sem, kv_sem,
     land_send, land_recv, ring_send, far2_recv, near2_recv, far1_recv, near1_recv, side_send, side_recv,
 ):
@@ -139,11 +144,14 @@
 
     wide = hidden_ref[...].astype(F32)
     inverse = lax.rsqrt(jnp.mean(wide * wide, axis=1, keepdims=True) + 1e-06)
-    normed = (wide * inverse * gain_ref[...].astype(F32)).astype(BF16)
+    gain = gain_ref[...].astype(F32)
     tables = routing_table(ids_ref, probs_ref)
     own_block = me.block(0, 0, 0)
-    for half in both:
-        gathered[half, own_block, :, 0:HALF] = normed[:, half * HALF : (half + 1) * HALF]
+    for part in range(D // TAIL):
+        half, low = divmod(part * TAIL, HALF)
+        normed = wide[:, part * TAIL : (part + 1) * TAIL] * inverse * gain[part : part + 1, :]
+        gathered[half, own_block, :, low : low + TAIL] = normed.astype(BF16)
+    for half in both:
         gathered[half, own_block, :, HALF:WIDE] = tables[half]
 
     experts = (
@@ -159,6 +167,7 @@
         wanted = jnp.where(slot_of // SLOTS == j, experts[j], wanted)
     pick_rank = jnp.where(lane == wanted, 1.0, 0.0).astype(BF16)
     pick_gate = jnp.where(lane == wanted + 64, 1.0, 0.0).astype(BF16)
+    pick_both = jnp.concatenate([pick_rank, pick_gate], axis=0)
 
     pl.semaphore_wait(barrier, len(neighbours))
 
@@ -196,6 +205,11 @@
         rank = lax.dot_general(pick_rank, table, (((1,), (1,)), ((), ())), preferred_element_type=F32)
         slot = (lax.broadcasted_iota(jnp.int32, (GROUPS * SLOTS, ROWS), 0) % SLOTS).astype(F32)
         hot = jnp.where(rank == slot, 1.0, 0.0).astype(BF16)
+        both_ways = lax.dot_general(table, pick_both, (((1,), (1,)), ((), ())), preferred_element_type=F32)
+        slot = (lax.broadcasted_iota(jnp.int32, (ROWS, GROUPS * SLOTS), 1) % SLOTS).astype(F32)
+        weights[half, block] = jnp.where(
+            both_ways[:, 0 : GROUPS * SLOTS] == slot, both_ways[:, GROUPS * SLOTS :], 0.0
+        ).astype(BF16)
         chosen = jnp.dot(hot, gathered[half, block, :, 0:HALF], preferred_element_type=F32).astype(BF16)
         columns = pl.ds(half * HALF, HALF)
         for core in range(2):
@@ -220,29 +234,31 @@
         for copy in cache_copies(chunk):
             copy.wait()
         scale = HEAD_DIM ** (-0.5)
-        position = lax.broadcasted_iota(jnp.int32, (16, KEYS), 1)
+        position = lax.broadcasted_iota(jnp.int32, (HEADS_HERE, KEYS), 1)
+        upper = lax.broadcasted_iota(jnp.int32, (HEADS_HERE, HEAD_DIM), 0) < HEADS_HERE // 2
+
+        def by_group(row):
+            return jnp.where(upper, row[:, 0:HEAD_DIM], row[:, HEAD_DIM:])
+
         for item in range(CHUNK):
             token = chunk * CHUNK + item
-            visible = position < lengths_ref[token]
-            for group in range(2):
-                heads = slice(group * 16, (group + 1) * 16)
-                lanes = slice(group * HEAD_DIM, (group + 1) * HEAD_DIM)
-                query = queries_ref[token, heads]
-                scores = lax.dot_general(
-                    query, keys[slot, item, :, lanes], (((1,), (1,)), ((), ())), preferred_element_type=F32
-                )
-                scores = jnp.where(visible, scores * scale, -1e30)
-                own_key = new_key_ref[token : token + 1, lanes].astype(F32)
-                own = jnp.sum(query.astype(F32) * own_key, axis=1, keepdims=True) * scale
-                top = jnp.maximum(jnp.max(scores, axis=1, keepdims=True), own)
-                scores = jnp.exp(scores - top)
-                own = jnp.exp(own - top)
-                total = jnp.sum(scores, axis=1, keepdims=True) + own
-                probs = (scores / total).astype(BF16)
-                own = (own / total).astype(BF16).astype(F32)
-                mixed = jnp.dot(probs, values[slot, item, :, lanes], preferred_element_type=F32)
-                mixed = mixed + own * new_value_ref[token : token + 1, lanes].astype(F32)
-                context_ref[token, heads] = mixed.astype(BF16)
+            heads = slice(token * HEADS_HERE, (token + 1) * HEADS_HERE)
+            query = query_rows[heads]
+            split = jnp.concatenate([jnp.where(upper, query, 0.0), jnp.where(upper, 0.0, query)], axis=1)
+            scores = lax.dot_general(
+                split.astype(BF16), keys[slot, item], (((1,), (1,)), ((), ())), preferred_element_type=F32
+            )
+            scores = jnp.where(position < lengths_ref[token], scores * scale, -1e30)
+            own_key = by_group(new_key_ref[token : token + 1, :].astype(F32))
+            own = jnp.sum(query * own_key, axis=1, keepdims=True) * scale
+            top = jnp.maximum(jnp.max(scores, axis=1, keepdims=True), own)
+            scores = jnp.exp(scores - top)
+            own = jnp.exp(own - top)
+            share = 1.0 / (jnp.sum(scores, axis=1, keepdims=True) + own)
+            probs = (scores * share).astype(BF16)
+            own = (own * share).astype(BF16).astype(F32)
+            mixed = by_group(jnp.dot(probs, values[slot, item], preferred_element_type=F32))
+            context_rows[heads] = mixed + own * by_group(new_value_ref[token : token + 1, :].astype(F32))
         if chunk + 2 < ROWS // CHUNK:
             for copy in cache_copies(chunk + 2):
                 copy.start()
@@ -253,6 +269,9 @@
         send_both(half, 0, 1, 4)
     for half in both:
         select(half, 0, 0)
+    for head in range(HEADS_HERE):
+        lanes = slice(head * HEAD_DIM, (head + 1) * HEAD_DIM)
+        query_rows[pl.ds(head, ROWS, stride=HEADS_HERE), :] = queries_ref[:, lanes].astype(F32)
     attend(0)
     for half in both:
         take_full(half, 0, 0, 0)
@@ -289,19 +308,11 @@
         select(half, 2, 2)
     attend(6)
 
-    for block in range(BLOCKS):
-        rank = lax.dot_general(
-            gathered[0, block, :, HALF:WIDE], pick_rank, (((1,), (1,)), ((), ())), preferred_element_type=F32
-        )
-        gate = sum(
-            lax.dot_general(
-                gathered[half, block, :, HALF:WIDE], pick_gate, (((1,), (1,)), ((), ())), preferred_element_type=F32
-            )
-            for half in both
-        )
-        slot = (lax.broadcasted_iota(jnp.int32, (ROWS, GROUPS * SLOTS), 1) % SLOTS).astype(F32)
-        weights[block] = jnp.where(rank == slot, gate, 0.0)
     attend(7)
+
+    for head in range(HEADS_HERE):
+        lanes = slice(head * HEAD_DIM, (head + 1) * HEAD_DIM)
+        context_ref[:, lanes] = context_rows[pl.ds(head, ROWS, stride=HEADS_HERE), :].astype(BF16)
 
     for copy in w_copies:
         copy.wait()
@@ -347,7 +358,7 @@
             device_id=me.sibling(), device_id_type=MESH,
         ).start()
 
-    AHEAD = 4
+    AHEAD = 6
     expert(lo * 2)
     for half in both:
         expert_down(lo * 2, half)
@@ -369,13 +380,12 @@
         turn[half] += 1
         block = me.block(half, first, second)
         landing(landed.at[half, block], land_recv.at[half, block])
-        weight = weights[block]
-        lead = weight.astype(BF16)
-        trail = (weight - lead.astype(F32)).astype(BF16)
         own = rows_out[own_group, block, :, pl.ds(half * HALF, HALF)]
         parts = landed[half, block]
         rows = jnp.concatenate([own, parts[0], parts[1], parts[2]], axis=0)
-        return jnp.dot(lead, rows, preferred_element_type=F32) + jnp.dot(trail, rows, preferred_element_type=F32)
+        return jnp.dot(weights[0, block], rows, preferred_element_type=F32) + jnp.dot(
+            weights[1, block], rows, preferred_element_type=F32
+        )
 
     def ring(half, stage, step, src, dst, sem):
         pltpu.make_async_remote_copy(
@@ -495,7 +505,7 @@
     context, moe_out = pl.pallas_call(
         step_kernel,
         out_shape=(
-            jax.ShapeDtypeStruct((ROWS, 32, HEAD_DIM), BF16),
+            jax.ShapeDtypeStruct((ROWS, HEADS_HERE * HEAD_DIM), BF16),
             jax.ShapeDtypeStruct((ROWS, D), BF16),
         ),
         in_specs=[vmem] * 4 + [smem] + [vmem] * 3 + [hbm] * 5,
@@ -505,7 +515,7 @@
             bf16(2, BLOCKS, 2, SLOTS, HALF),
             bf16(2, BLOCKS, SLOTS, HALF),
             bf16(GROUPS, BLOCKS, SLOTS, D),
-            pltpu.VMEM((BLOCKS, ROWS, GROUPS * SLOTS), F32),
+            bf16(2, BLOCKS, ROWS, GROUPS * SLOTS),
             bf16(D, HIDDEN),
             bf16(D, HIDDEN),
             bf16(HIDDEN, D),
@@ -524,6 +534,8 @@
             bf16(2, ROWS, HALF),
             bf16(2, CHUNK, KEYS, 2 * HEAD_DIM),
             bf16(2, CHUNK, KEYS, 2 * HEAD_DIM),
+            pltpu.VMEM((ROWS * HEADS_HERE, HEAD_DIM), F32),
+            pltpu.VMEM((ROWS * HEADS_HERE, HEAD_DIM), F32),
             dma, dma((2, 20)), dma, dma, dma((3,)), dma((2, 2)),
             dma, dma((2, BLOCKS)), dma, dma((2, 4, 2)), dma((2, 4, 2)), dma((2, 2)), dma((2, 2)), dma, dma((2,)),
         ],
@@ -532,11 +544,11 @@
         ),
         name="step",
     )(
-        hidden, norm_gain.reshape(1, D), expert_ids, router_probs, cache_lengths,
-        queries.reshape(ROWS, 32, HEAD_DIM), new_key, new_value,
+        hidden, norm_gain.reshape(D // TAIL, TAIL), expert_ids.T, router_probs.T, cache_lengths,
+        queries, new_key, new_value,
         cache_keys, cache_values, w_gate[0], w_up[0], w_down[0],
     )
-    return (context.reshape(ROWS, 32 * HEAD_DIM), moe_out)
+    return (context, moe_out)
 
 
 def solution(mesh):

time: 103 us -> 90.4 us (0.88)
  local copies, waits for them, and re-layouts: 9.17 us -> 3.34 us
  Pallas kernels: 92 us -> 86.2 us
    pallas_call x1, Pallas kernels: 92 us -> 86.2 us  [per_device(): pl.pallas_call(step_kernel, out_shape=(jax.ShapeDtypeStruct((ROWS, HEADS_...]
    unnamed x5 -> x2, local copies, waits for them, and re-layouts: 7.85 us -> 3.34 us
    reshape x1 -> x0, local copies, waits for them, and re-layouts: 1.31 us -> none  [per_device(): norm_gain.reshape(1, D)]
where the time goes in v3:
time: 90.4 us; the launch traced here: 90.2 us
  Pallas kernels  86.2 us (95%)
  local copies, waits for them, and re-layouts  3.34 us (4%)
    pallas_call x1, Pallas kernels, per_device(): pl.pallas_call(step_kernel, out_shape=(jax.ShapeDtypeStruct((ROWS, HEADS_...  86.2 us
    unnamed x2, local copies, waits for them, and re-layouts  3.34 us

profile of v3, /device:TPU:2, one launch (start us, length us, event | category | flops | bytes accessed | tf_op | source)
XLA Modules:
  0.0 90.2 jit_solution(10873213854366461263)
XLA Ops:
  0.6 86.2 %step.1 = (bf16[32,4096]{1,0:T(8,128)(2,1)}, bf16[32,4096]{1,0:T(8,128)(2,1)}) custom-call(bf16[32,4096]{1,0:T(8,128)(2,1)} %hidden_ref.1, bf16[32,128]{1,0:T(8,128)(2,1)} %bitcast.9, s32[8,32]{1,0:T(8,128)} %bitcast.10, f32[8,32]{1,0:T(8,128)} %bitcast.11, s32[32]{0:T(128)} %lengths_ref.1, bf16[32,4096]{1,0:T(8,128)(2,1)} %queries_ref.1, ...), custom_call_target="tpu_custom_call" | custom-call | tf_op jit(solution)/shard_map/step/pallas_call | solution.py:505
  86.9 1.7 %copy.17 = bf16[32,4096]{1,0:T(8,128)(2,1)} copy(bf16[32,4096]{1,0:T(8,128)(2,1)} %get-tuple-element.4) | data formatting | bytes 524288
  88.5 1.7 %copy.18 = bf16[32,4096]{1,0:T(8,128)(2,1)} copy(bf16[32,4096]{1,0:T(8,128)(2,1)} %get-tuple-element.5) | data formatting | bytes 524288

commit v4 on v3

--- a/solution.py
+++ b/solution.py
@@ -61,6 +61,14 @@
 
 AXES = (("x", "z"), ("z", "x"))
 NEAR = (0, -1, 1, 2)
+LISTED = (
+    (2, 2), (1, 2), (2, 1), (-1, 2), (2, -1), (1, 1), (0, 2), (2, 0),
+    (1, -1), (-1, 1), (-1, -1), (0, 1), (1, 0), (0, -1), (-1, 0), (0, 0),
+)
+
+
+def listed(half, first, second):
+    return LISTED.index((first, second) if half == 0 else (second, first))
 
 
 def routing_table(ids_ref, probs_ref):
@@ -207,27 +215,28 @@
         hot = jnp.where(rank == slot, 1.0, 0.0).astype(BF16)
         both_ways = lax.dot_general(table, pick_both, (((1,), (1,)), ((), ())), preferred_element_type=F32)
         slot = (lax.broadcasted_iota(jnp.int32, (ROWS, GROUPS * SLOTS), 1) % SLOTS).astype(F32)
-        weights[half, block] = jnp.where(
+        weights[half, listed(half, first, second)] = jnp.where(
             both_ways[:, 0 : GROUPS * SLOTS] == slot, both_ways[:, GROUPS * SLOTS :], 0.0
         ).astype(BF16)
         chosen = jnp.dot(hot, gathered[half, block, :, 0:HALF], preferred_element_type=F32).astype(BF16)
         columns = pl.ds(half * HALF, HALF)
+        place = listed(half, first, second)
         for core in range(2):
             picked_y[half, block, core] = chosen[16 + 8 * core : 24 + 8 * core]
             pltpu.make_async_remote_copy(
                 src_ref=picked_y.at[half, block, core],
-                dst_ref=rows_in.at[own_group, block, :, columns],
-                send_sem=pick_send, recv_sem=rows_recv,
+                dst_ref=rows_in.at[own_group, place, :, columns],
+                send_sem=pick_send, recv_sem=rows_recv.at[1],
                 device_id=me.along_y(1 if half == 0 else -1, core), device_id_type=MESH,
             ).start()
         picked_s[half, block] = chosen[8:16]
         pltpu.make_async_remote_copy(
             src_ref=picked_s.at[half, block],
-            dst_ref=rows_in.at[own_group, block, :, columns],
-            send_sem=pick_send, recv_sem=rows_recv,
+            dst_ref=rows_in.at[own_group, place, :, columns],
+            send_sem=pick_send, recv_sem=rows_recv.at[0],
             device_id=me.sibling(), device_id_type=MESH,
         ).start()
-        rows_in[own_group, block, :, columns] = chosen[0:8]
+        rows_in[own_group, place, :, columns] = chosen[0:8]
 
     def attend(chunk):
         slot = chunk % 2
@@ -306,31 +315,21 @@
     for half in both:
         take_far(half, 2, 1, 16)
         select(half, 2, 2)
-    attend(6)
-
-    attend(7)
-
-    for head in range(HEADS_HERE):
-        lanes = slice(head * HEAD_DIM, (head + 1) * HEAD_DIM)
-        context_ref[:, lanes] = context_rows[pl.ds(head, ROWS, stride=HEADS_HERE), :].astype(BF16)
-
-    for copy in w_copies:
-        copy.wait()
-    landing(rows_in.at[pl.ds(0, 3)], rows_recv)
-
-    def expert(base):
-        rows = rows_in[pl.ds(base, 2)].reshape(2 * BLOCKS * SLOTS, D)
+    PART = BLOCKS // 2
+
+    def expert(base, part):
+        rows = rows_in[pl.ds(base, 2), part * PART : (part + 1) * PART].reshape(2 * PART * SLOTS, D)
         for low in range(0, HIDDEN, 256):
             columns = slice(low, low + 256)
             gate = jnp.dot(rows, w_gate[:, columns], preferred_element_type=F32)
             up = jnp.dot(rows, w_up[:, columns], preferred_element_type=F32)
             active[:, columns] = (gate / (1.0 + jnp.exp(-gate)) * up).astype(BF16)
 
-    def expert_down(base, half):
+    def expert_down(base, part, half):
         for low in range(half * HALF, (half + 1) * HALF, 512):
             columns = slice(low, low + 512)
             out = jnp.dot(active[...], w_down[:, columns], preferred_element_type=F32).astype(BF16)
-            rows_out[pl.ds(base, 2), :, :, columns] = out.reshape(2, BLOCKS, SLOTS, 512)
+            rows_out[pl.ds(base, 2), part * PART : (part + 1) * PART, :, columns] = out.reshape(2, PART, SLOTS, 512)
 
     far_order = (2, 1, -1, 0)
     visits = (
@@ -339,36 +338,43 @@
     )
 
     def give_y(half, visit):
-        block = me.block(half, *visits[visit])
+        place = listed(half, *visits[visit])
         columns = pl.ds(half * HALF, HALF)
         for core in range(2):
             pltpu.make_async_remote_copy(
-                src_ref=rows_out.at[lo * 2 + core, block, :, columns],
-                dst_ref=landed.at[half, block, 1 + me.core],
-                send_sem=land_send, recv_sem=land_recv.at[half, block],
+                src_ref=rows_out.at[lo * 2 + core, place, :, columns],
+                dst_ref=landed.at[half, visit, 1 + me.core],
+                send_sem=land_send, recv_sem=land_recv.at[half, visit],
                 device_id=me.along_y(1 if half == 0 else -1, core), device_id_type=MESH,
             ).start()
 
     def give_sibling(half, visit):
-        block = me.block(half, *visits[visit])
+        place = listed(half, *visits[visit])
         pltpu.make_async_remote_copy(
-            src_ref=rows_out.at[me.lo * 2 + 1 - me.core, block, :, pl.ds(half * HALF, HALF)],
-            dst_ref=landed.at[half, block, 0],
-            send_sem=land_send, recv_sem=land_recv.at[half, block],
+            src_ref=rows_out.at[me.lo * 2 + 1 - me.core, place, :, pl.ds(half * HALF, HALF)],
+            dst_ref=landed.at[half, visit, 0],
+            send_sem=land_send, recv_sem=land_recv.at[half, visit],
             device_id=me.sibling(), device_id_type=MESH,
         ).start()
 
     AHEAD = 6
-    expert(lo * 2)
-    for half in both:
-        expert_down(lo * 2, half)
+    for copy in w_copies:
+        copy.wait()
+    landing(rows_in.at[0], rows_recv.at[0])
+    expert(me.lo * 2, 0)
+    for half in both:
+        expert_down(me.lo * 2, 0, half)
+    landing(rows_in.at[pl.ds(0, 2)], rows_recv.at[1])
+    expert(lo * 2, 0)
+    for half in both:
+        expert_down(lo * 2, 0, half)
         for visit in range(AHEAD):
             give_y(half, visit)
-    expert(me.lo * 2)
-    for half in both:
-        expert_down(me.lo * 2, half)
-        for visit in range(AHEAD):
             give_sibling(half, visit)
+    for base in (lo * 2, me.lo * 2):
+        expert(base, 1)
+        for half in both:
+            expert_down(base, 1, half)
 
     turn = [0, 0]
 
@@ -377,14 +383,15 @@
         if turn[half] + AHEAD < BLOCKS:
             give_y(half, turn[half] + AHEAD)
             give_sibling(half, turn[half] + AHEAD)
+        visit = turn[half]
         turn[half] += 1
-        block = me.block(half, first, second)
-        landing(landed.at[half, block], land_recv.at[half, block])
-        own = rows_out[own_group, block, :, pl.ds(half * HALF, HALF)]
-        parts = landed[half, block]
+        place = listed(half, first, second)
+        landing(landed.at[half, visit], land_recv.at[half, visit])
+        own = rows_out[own_group, place, :, half * HALF : (half + 1) * HALF]
+        parts = landed[half, visit]
         rows = jnp.concatenate([own, parts[0], parts[1], parts[2]], axis=0)
-        return jnp.dot(weights[0, block], rows, preferred_element_type=F32) + jnp.dot(
-            weights[1, block], rows, preferred_element_type=F32
+        return jnp.dot(weights[0, place], rows, preferred_element_type=F32) + jnp.dot(
+            weights[1, place], rows, preferred_element_type=F32
         )
 
     def ring(half, stage, step, src, dst, sem):
@@ -462,6 +469,13 @@
         if index > 0:
             for half in both:
                 stage1(half, index - 1)
+        if index == 1:
+            attend(6)
+        elif index == 2:
+            attend(7)
+    for head in range(HEADS_HERE):
+        lanes = slice(head * HEAD_DIM, (head + 1) * HEAD_DIM)
+        context_ref[:, lanes] = context_rows[pl.ds(head, ROWS, stride=HEADS_HERE), :].astype(BF16)
     for half in both:
         stage1(half, 3)
     for half in both:
@@ -477,6 +491,11 @@
     for ref in (far2_out, near2_out, far1_out, near1_out):
         landing(ref, ring_send)
     landing(side_out, side_send)
+
+
+def hand_over_kernel(context_in, moe_in, context_out, moe_out):
+    context_out[...] = context_in[...]
+    moe_out[...] = moe_in[...]
 
 
 def per_device(
@@ -519,7 +538,7 @@
             bf16(D, HIDDEN),
             bf16(D, HIDDEN),
             bf16(HIDDEN, D),
-            bf16(2 * BLOCKS * SLOTS, HIDDEN),
+            bf16(BLOCKS * SLOTS, HIDDEN),
             bf16(GROUPS, BLOCKS, SLOTS, D),
             bf16(2, BLOCKS, 3, SLOTS, HALF),
             bf16(2, 4, ROWS, HALF),
@@ -536,7 +555,7 @@
             bf16(2, CHUNK, KEYS, 2 * HEAD_DIM),
             pltpu.VMEM((ROWS * HEADS_HERE, HEAD_DIM), F32),
             pltpu.VMEM((ROWS * HEADS_HERE, HEAD_DIM), F32),
-            dma, dma((2, 20)), dma, dma, dma((3,)), dma((2, 2)),
+            dma, dma((2, 20)), dma, dma((2,)), dma((3,)), dma((2, 2)),
             dma, dma((2, BLOCKS)), dma, dma((2, 4, 2)), dma((2, 4, 2)), dma((2, 2)), dma((2, 2)), dma, dma((2,)),
         ],
         compiler_params=pltpu.CompilerParams(
@@ -548,7 +567,13 @@
         queries, new_key, new_value,
         cache_keys, cache_values, w_gate[0], w_up[0], w_down[0],
     )
-    return (context, moe_out)
+    return pl.pallas_call(
+        hand_over_kernel,
+        out_shape=(jax.ShapeDtypeStruct(context.shape, BF16), jax.ShapeDtypeStruct(moe_out.shape, BF16)),
+        in_specs=[vmem] * 2,
+        out_specs=(vmem, vmem),
+        name="hand_over",
+    )(context, moe_out)
 
 
 def solution(mesh):

time: 90.4 us -> 86.1 us (0.952)
  local copies, waits for them, and re-layouts: 3.34 us -> 0 us
    unnamed x2 -> x0, local copies, waits for them, and re-layouts: 3.34 us -> none
    pallas_call x1, Pallas kernels: 86.2 us -> 83.4 us  [per_device(): pl.pallas_call(step_kernel, out_shape=(jax.ShapeDtypeStruct((ROWS, HEADS_...]
    pallas_call x0 -> x1, Pallas kernels: none -> 1.84 us  [per_device(): pl.pallas_call(hand_over_kernel, out_shape=(jax.ShapeDtypeStruct(context....]
where the time goes in v4:
time: 86.1 us; the launch traced here: 85.9 us
  Pallas kernels  85.3 us (99%)
    pallas_call x1, Pallas kernels, per_device(): pl.pallas_call(step_kernel, out_shape=(jax.ShapeDtypeStruct((ROWS, HEADS_...  83.4 us
    pallas_call x1, Pallas kernels, per_device(): pl.pallas_call(hand_over_kernel, out_shape=(jax.ShapeDtypeStruct(context....  1.84 us

profile of v4, /device:TPU:2, one launch (start us, length us, event | category | flops | bytes accessed | tf_op | source)
XLA Modules:
  0.0 85.9 jit_solution(2418424153639486136)
XLA Ops:
  0.6 83.4 %step.1 = (bf16[32,4096]{1,0:T(8,128)(2,1)}, bf16[32,4096]{1,0:T(8,128)(2,1)}) custom-call(bf16[32,4096]{1,0:T(8,128)(2,1)} %hidden_ref.1, bf16[32,128]{1,0:T(8,128)(2,1)} %bitcast.9, s32[8,32]{1,0:T(8,128)} %bitcast.10, f32[8,32]{1,0:T(8,128)} %bitcast.11, s32[32]{0:T(128)} %lengths_ref.1, bf16[32,4096]{1,0:T(8,128)(2,1)} %queries_ref.1, ...), custom_call_target="tpu_custom_call" | custom-call | tf_op jit(solution)/shard_map/step/pallas_call | solution.py:524
  84.1 1.8 %hand_over.1 = (bf16[32,4096]{1,0:T(8,128)(2,1)}, bf16[32,4096]{1,0:T(8,128)(2,1)}) custom-call(bf16[32,4096]{1,0:T(8,128)(2,1)} %get-tuple-element.4.context_in, bf16[32,4096]{1,0:T(8,128)(2,1)} %get-tuple-element.5.moe_in), custom_call_target="tpu_custom_call" | custom-call | tf_op jit(solution)/shard_map/hand_over/pallas_call | solution.py:570

commit v5 on v4

--- a/solution.py
+++ b/solution.py
@@ -282,13 +282,14 @@
         lanes = slice(head * HEAD_DIM, (head + 1) * HEAD_DIM)
         query_rows[pl.ds(head, ROWS, stride=HEADS_HERE), :] = queries_ref[:, lanes].astype(F32)
     attend(0)
+    attend(1)
     for half in both:
         take_full(half, 0, 0, 0)
         send_both(half, -1, 1, 8)
     for half in both:
         select(half, -1, 0)
         select(half, 1, 0)
-    attend(1)
+    attend(2)
     for half in both:
         take_full(half, 0, 1, 4)
         send_both(half, 1, 1, 12)
@@ -298,7 +299,7 @@
         select(half, 2, 0)
         select(half, 0, -1)
         select(half, 0, 1)
-    attend(2)
+    attend(3)
     for index in range(1, 4):
         first = NEAR[index]
         for half in both:
@@ -311,7 +312,8 @@
             select(half, first, -1)
             select(half, first, 1)
             select(half, NEAR[index - 1], 2)
-        attend(2 + index)
+        if index < 3:
+            attend(3 + index)
     for half in both:
         take_far(half, 2, 1, 16)
         select(half, 2, 2)

time: 86.1 us -> 86.1 us (level)
  no operation moved by 1% of the time
where the time goes in v5:
time: 86.1 us; the launch traced here: 85.9 us
  Pallas kernels  85.3 us (99%)
    pallas_call x1, Pallas kernels, per_device(): pl.pallas_call(step_kernel, out_shape=(jax.ShapeDtypeStruct((ROWS, HEADS_...  83.5 us
    pallas_call x1, Pallas kernels, per_device(): pl.pallas_call(hand_over_kernel, out_shape=(jax.ShapeDtypeStruct(context....  1.84 us

profile of v5, /device:TPU:2, one launch (start us, length us, event | category | flops | bytes accessed | tf_op | source)
XLA Modules:
  0.0 85.9 jit_solution(2733457218115018323)
XLA Ops:
  0.6 83.5 %step.1 = (bf16[32,4096]{1,0:T(8,128)(2,1)}, bf16[32,4096]{1,0:T(8,128)(2,1)}) custom-call(bf16[32,4096]{1,0:T(8,128)(2,1)} %hidden_ref.1, bf16[32,128]{1,0:T(8,128)(2,1)} %bitcast.9, s32[8,32]{1,0:T(8,128)} %bitcast.10, f32[8,32]{1,0:T(8,128)} %bitcast.11, s32[32]{0:T(128)} %lengths_ref.1, bf16[32,4096]{1,0:T(8,128)(2,1)} %queries_ref.1, ...), custom_call_target="tpu_custom_call" | custom-call | tf_op jit(solution)/shard_map/step/pallas_call | solution.py:526
  84.1 1.8 %hand_over.1 = (bf16[32,4096]{1,0:T(8,128)(2,1)}, bf16[32,4096]{1,0:T(8,128)(2,1)}) custom-call(bf16[32,4096]{1,0:T(8,128)(2,1)} %get-tuple-element.4.context_in, bf16[32,4096]{1,0:T(8,128)(2,1)} %get-tuple-element.5.moe_in), custom_call_target="tpu_custom_call" | custom-call | tf_op jit(solution)/shard_map/hand_over/pallas_call | solution.py:572
